TPU v7x, 128 devices: a whole 4x4x4 slice. The times are simulated.
128 devices in a mesh: ctx: 16 (over y, z_hi, core), dp: 8 (over x, z_lo).
Axes of the slice: x: 4, y: 4, z: 4 (z_hi: 2, z_lo: 2; z = z_hi * 2 + z_lo), core: 2. Of those that a mesh axis runs over, the one named last changes fastest.
Arguments:
- tokens: bfloat16 [8, 4096, 16384], P('dp', 'ctx'), may hold values from -6 to 6
- queries: bfloat16 [8, 4096, 1024], P('dp', 'ctx'), may hold values from -200 to 200
- cotangent: bfloat16 [8, 4096, 1024], P('dp', 'ctx'), may hold values from -6 to 6
- latent_key: float32 [16384, 128], P(('ctx', 'dp')), may hold values from -1 to 1
- latent_value: float32 [16384, 128], P(('ctx', 'dp')), may hold values from -1 to 1
- lengths: int32 [8, 8], P('dp'), may hold values from 1 to 2048, 4096 in all within a row
- block_order: int32 [8, 32], P('dp'), may hold values from 0 to 31, each once within a row
Outputs:
- attn_out: bfloat16 [8, 4096, 1024], P('dp', 'ctx')
- query_grad: bfloat16 [8, 4096, 1024], P('dp', 'ctx')
- token_grad: bfloat16 [8, 4096, 16384], P('dp', 'ctx')
- key_weight_grad: float32 [16384, 128], P(('ctx', 'dp'))
- value_weight_grad: float32 [16384, 128], P(('ctx', 'dp'))
Inputs may be any that keep to these rules, and one draw needn't show every extreme that they name: Each row holds the lengths of the 8 documents packed into one sequence, in order; they sum to 4096 and the largest is exactly 2048. Each row is a permutation; stored block b of a sequence (rows b * 128 to (b + 1) * 128 - 1) holds the tokens at positions block_order[b] * 128 to block_order[b] * 128 + 127.
All inputs are finite; a program needn't handle non-finite values. Where the computation divides by a largest or mean magnitude, that divisor is 1e-20 or more.
Results may differ from a plain program's by a relative error of at most 0.02.
The roundings to bfloat16 on the way count: a program that leaves them out, or rounds other values in their place, can miss the bound.
Values may be sent and summed in bfloat16 or wider, within the bound.
No kernel may reach another device: no remote copies, remote signals or barrier semaphores. Data moves between devices by JAX's collectives and lax.ppermute only.
A program may use at most 128 MiB of HBM per device.

v0:
```python
import jax
import jax.numpy as jnp
from jax import lax
from jax.sharding import Mesh
from jax.sharding import PartitionSpec as P

CTX = ("ctx_0", "ctx_1", "ctx_2")
CTX_DP = ("ctx_0", "ctx_1", "ctx_2", "dp_0", "dp_1")
DP = ("dp_0", "dp_1")


EPSILON = 1e-05
NEGATIVE = -1e30


def over_axes(value, axes):
    for axis in axes:
        value = lax.psum(value, axis)
    return value


def in_one_piece(arrays, axis, dim, along):
    both = jnp.concatenate(arrays, axis=along)
    result, at, done = (lax.all_gather(both, axis, axis=dim, tiled=True), 0, [])
    for a in arrays:
        done.append(lax.slice_in_dim(result, at, at + a.shape[along], axis=along))
        at += a.shape[along]
    return tuple(done)


def levels(ratio):
    return jnp.where(ratio >= 0.5, 1.0, jnp.where(ratio <= -0.5, -1.0, 0.0)).astype(jnp.float32)


def over_blocks(advance, state_now, key_rows, value_rows):
    row_total = key_rows.shape[0]
    width_rows = 512
    block_count = row_total // width_rows
    key_blocks = key_rows.reshape(block_count, width_rows, key_rows.shape[1])
    value_blocks = value_rows.reshape(block_count, width_rows, value_rows.shape[1])

    def turn_once(carried, block_item):
        key_block, value_block, number = block_item
        return (advance(carried, key_block, value_block, number * width_rows), None)

    state_now, _ = lax.scan(
        turn_once, state_now, (key_blocks, value_blocks, jnp.arange(block_count, dtype=jnp.int32))
    )
    return state_now


def body(tokens, queries, cotangent, latent_key, latent_value, lengths, block_order):
    token_rows = tokens[0]
    rows_here = token_rows.shape[0]
    head_size = latent_key.shape[1]
    head_count = queries.shape[2] // head_size
    scale_factor = head_size ** (-0.5)
    block_rows = rows_here // 2
    lengths_row = lengths[0]
    order_row = block_order[0]
    block_ids = jnp.arange(order_row.shape[0], dtype=jnp.int32)
    doc_starts = jnp.cumsum(lengths_row, dtype=jnp.int32) - lengths_row

    def positions(stored):
        owner = jnp.sum(
            jnp.where((stored // block_rows)[:, None] == block_ids[None, :], order_row[None, :], 0),
            axis=1,
        )
        return owner * block_rows + stored % block_rows

    def documents(position):
        return jnp.sum((position[:, None] >= doc_starts[None, :]).astype(jnp.int32), axis=1)

    query_pos = positions(lax.axis_index(CTX) * rows_here + jnp.arange(rows_here, dtype=jnp.int32))
    query_doc = documents(query_pos)

    def visibility(first_row, row_total):
        key_pos = positions(first_row + jnp.arange(row_total, dtype=jnp.int32))
        key_doc = documents(key_pos)
        return (key_pos[None, :] <= query_pos[:, None]) & (key_doc[None, :] == query_doc[:, None])

    entry_count = latent_key.shape[0] * lax.axis_size(CTX_DP) * head_size
    magnitudes = (
        over_axes(jnp.sum(jnp.abs(latent_key)), CTX_DP),
        over_axes(jnp.sum(jnp.abs(latent_value)), CTX_DP),
    )
    key_scale = magnitudes[0] / entry_count + EPSILON
    value_scale = magnitudes[1] / entry_count + EPSILON
    local_rows = jnp.concatenate(
        [
            (key_scale * levels(latent_key / key_scale)).astype(jnp.bfloat16),
            (value_scale * levels(latent_value / value_scale)).astype(jnp.bfloat16),
        ],
        axis=1,
    )
    both = lax.all_gather(local_rows, CTX_DP, axis=0, tiled=True)
    projected = jnp.dot(token_rows, both, preferred_element_type=jnp.float32).astype(jnp.bfloat16)
    key_pair = (projected[:, :head_size][None], projected[:, head_size:][None])
    query_heads = queries[0].reshape(rows_here, head_count, head_size)
    cot_heads = cotangent[0].reshape(rows_here, head_count, head_size)

    def forward_block(state_now, key_block, value_block, first_row):
        best, total, accum = state_now
        scores = (
            jnp.einsum("thd,sd->hts", query_heads, key_block, preferred_element_type=jnp.float32)
            * scale_factor
        )
        visible = visibility(first_row, key_block.shape[0])
        scores = jnp.where(visible[None], scores, NEGATIVE)
        new_best = jnp.maximum(best, jnp.max(scores, axis=2))
        weights = jnp.where(visible[None], jnp.exp(scores - new_best[:, :, None]), 0.0)
        shrink = jnp.exp(best - new_best)
        total = total * shrink + jnp.sum(weights, axis=2)
        accum = accum * shrink.T[:, :, None] + jnp.einsum(
            "hts,sd->thd",
            weights.astype(jnp.bfloat16),
            value_block,
            preferred_element_type=jnp.float32,
        )
        return (new_best, total, accum)

    start_state = (
        jnp.full((head_count, rows_here), NEGATIVE, jnp.float32),
        jnp.zeros((head_count, rows_here), jnp.float32),
        jnp.zeros((rows_here, head_count, head_size), jnp.float32),
    )
    shard_part = in_one_piece((key_pair[0], key_pair[1]), CTX, 1, 0)
    state_final = over_blocks(forward_block, start_state, shard_part[0][0], shard_part[1][0])
    all_keys, all_values = in_one_piece((key_pair[0], key_pair[1]), CTX, 1, 0)
    best, total, accum = state_final
    log_total = best + jnp.log(total)
    mixed = (accum / total.T[:, :, None]).astype(jnp.bfloat16)
    expected = jnp.sum(cot_heads.astype(jnp.float32) * mixed.astype(jnp.float32), axis=2).T

    def backward_block(query_acc, key_block, value_block, first_row):
        scores = (
            jnp.einsum("thd,sd->hts", query_heads, key_block, preferred_element_type=jnp.float32)
            * scale_factor
        )
        visible = visibility(first_row, key_block.shape[0])
        probability = jnp.where(visible[None], jnp.exp(scores - log_total[:, :, None]), 0.0)
        prob_grad = jnp.einsum(
            "thd,sd->hts", cot_heads, value_block, preferred_element_type=jnp.float32
        )
        score_grad = (probability * (prob_grad - expected[:, :, None])).astype(jnp.bfloat16)
        query_acc = (
            query_acc
            + jnp.einsum("hts,sd->thd", score_grad, key_block, preferred_element_type=jnp.float32)
            * scale_factor
        )
        key_part = (
            jnp.einsum("hts,thd->sd", score_grad, query_heads, preferred_element_type=jnp.float32)
            * scale_factor
        )
        value_part = jnp.einsum(
            "hts,thd->sd",
            probability.astype(jnp.bfloat16),
            cot_heads,
            preferred_element_type=jnp.float32,
        )
        return (query_acc, jnp.concatenate([key_part, value_part], axis=1))

    key_all = all_keys[0]
    value_all = all_values[0]
    total_rows = key_all.shape[0]
    width_rows = 512
    block_count = total_rows // width_rows

    def backward_turn(query_acc, block_item):
        key_block, value_block, number = block_item
        return backward_block(query_acc, key_block, value_block, number * width_rows)

    query_acc, key_terms = lax.scan(
        backward_turn,
        jnp.zeros((rows_here, head_count, head_size), jnp.float32),
        (
            key_all.reshape(block_count, width_rows, head_size),
            value_all.reshape(block_count, width_rows, head_size),
            jnp.arange(block_count, dtype=jnp.int32),
        ),
    )
    key_terms = key_terms.reshape(total_rows, 2 * head_size)
    grads_kv = lax.psum_scatter(key_terms, CTX, scatter_dimension=0, tiled=True).astype(
        jnp.bfloat16
    )
    token_grad = lax.dot_general(
        grads_kv, both, (((1,), (1,)), ((), ())), preferred_element_type=jnp.float32
    ).astype(jnp.bfloat16)
    columns_all = lax.all_to_all(token_rows, CTX_DP, split_axis=1, concat_axis=0, tiled=True)
    summed = lax.dot_general(
        columns_all,
        lax.all_gather(grads_kv, CTX_DP, axis=0, tiled=True),
        (((0,), (0,)), ((), ())),
        preferred_element_type=jnp.float32,
    )
    key_weight_grad = summed[:, :head_size]
    value_weight_grad = summed[:, head_size:]
    attn_out = mixed.reshape(rows_here, head_count * head_size)[None]
    query_grad = query_acc.astype(jnp.bfloat16).reshape(rows_here, head_count * head_size)[None]
    return (attn_out, query_grad, token_grad[None], key_weight_grad, value_weight_grad)


def solution(mesh):
    torus = Mesh(mesh.devices.reshape(4, 2, 2, 4, 2), ("ctx_0", "ctx_1", "ctx_2", "dp_0", "dp_1"))
    in_specs = (
        P(DP, CTX, None),
        P(DP, CTX, None),
        P(DP, CTX, None),
        P(CTX_DP, None),
        P(CTX_DP, None),
        P(DP, None),
        P(DP, None),
    )
    out_specs = (
        P(DP, CTX, None),
        P(DP, CTX, None),
        P(DP, CTX, None),
        P(CTX_DP, None),
        P(CTX_DP, None),
    )
    return jax.shard_map(body, mesh=torus, in_specs=in_specs, out_specs=out_specs, check_vma=False)
```

profile of v0, /device:TPU:0, one launch (start us, length us, event | category | flops | bytes accessed | tf_op | source)
XLA Modules:
  0.0 1080.9 jit_solution(9353580749844137275)
XLA Ops:
  8.7 11.4 %all-reduce.1 = (f32[]{:T(128)}, f32[]{:T(128)}) all-reduce(f32[]{:T(128)} %get-tuple-element.651, f32[]{:T(128)} %get-tuple-element.652), channel_id=1, replica_groups=mesh['ctx_0'=4,'ctx_1'=2,'ctx_2'=2,'dp_0'=4,'dp_1'=2] {'ctx_0'}, use_global_device_ids=true, to_apply=%region_7.8 | all-reduce | flops 2 | bytes 16 | tf_op jit(solution)/shard_map/psum | solution.py:18
  20.1 7.4 all-reduce.4
  27.5 3.1 all-reduce.3
  30.6 11.1 %all-reduce = (f32[]{:T(128)}, f32[]{:T(128)}) all-reduce(f32[]{:T(128)} %get-tuple-element.635, f32[]{:T(128)} %get-tuple-element.636), channel_id=1, replica_groups=mesh['ctx_0'=4,'ctx_1'=2,'ctx_2'=2,'dp_0'=4,'dp_1'=2] {'dp_0'}, use_global_device_ids=true, to_apply=%region_10.11 | all-reduce | flops 2 | bytes 16 | tf_op jit(solution)/shard_map/psum | solution.py:18
  41.7 5.6 all-reduce.2
  51.1 308.9 %all-gather.4.cloned.1.call-done = bf16[16384,256]{1,0:T(8,128)(2,1)} async-done(((bf16[128,256]{1,0:T(8,128)(2,1)}), bf16[16384,256]{1,0:T(8,128)(2,1)}) %all-gather.4.cloned.1.call-update) | async-done | bytes 8388624 | tf_op jit(solution)/shard_map/all_gather | solution.py:96
  360.0 8.1 fusion.68
  371.1 48.8 %all-gather.6.cloned.1.call-done = bf16[2,4096,128]{1,2,0:T(8,128)(2,1)} async-done(((bf16[2,256,128]{1,2,0:T(8,128)(2,1)}), bf16[2,4096,128]{1,2,0:T(8,128)(2,1)}) %all-gather.6.cloned.1.call-update) | async-done | bytes 2097168 | tf_op jit(solution)/shard_map/all_gather | solution.py:24
  419.8 2.7 fusion.74
  428.2 62.8 %while.32 = (s32[]{:T(128)}, f32[8,256]{1,0:T(8,128)S(1)}, f32[8,256]{1,0:T(8,128)S(1)}, f32[256,8,128]{0,2,1:T(8,128)}, s32[8]{0:T(128)S(1)}, /*index=5*/s32[1,...) while((s32[]{:T(128)}, f32[8,256]{1,0:T(8,128)S(1)}, ...), condition=%wide.region_20.21_spmd.clone, body=%wide.region_15.20_spmd.clone.sunk | while | flops 551770112 | bytes 24531360 | solution.py:46
  432.7 2.4 fusion.121
  440.6 2.4 fusion.121
  448.4 2.4 fusion.121
  472.0 2.4 fusion.121
  479.8 2.4 fusion.121
  487.7 2.4 fusion.121
  493.2 80.0 %while.33 = (s32[]{:T(128)}, f32[256,8,128]{0,2,1:T(8,128)S(1)}, f32[8,512,256]{2,1,0:T(8,128)}, bf16[8,512,128]{2,1,0:T(8,128)(2,1)}, s32[8]{0:T(128)S(1)}, /*i...) while((s32[]{:T(128)}, f32[256,8,128]{0,2,1:T(8,128)S(1)}, ...), condition=%wide.region_25.26_spmd.clone, body=%wide.region_22.25_spmd.clone.sunk | while | flops 1354115072 | bytes 27570560 | solution.py:173
  573.3 79.2 %reduce-scatter.2.cloned.1.call-done = f32[256,256]{1,0:T(8,128)} async-done(((f32[4096,256]{1,0:T(8,128)}), f32[256,256]{1,0:T(8,128)}) %reduce-scatter.2.cloned.1.call-update) | async-done | bytes 262160 | tf_op jit(solution)/shard_map/reduce_scatter | solution.py:183
  654.2 11.9 %copy.87 = bf16[1,256,16384]{1,2,0:T(8,128)(2,1)} copy(bf16[1,256,16384]{2,1,0:T(8,128)(2,1)} %param.11) | data formatting | bytes 16777216 | tf_op args[0]
  666.1 113.4 %all_to_all.19 = bf16[256,128,128]{0,2,1:T(8,128)(2,1)} all-to-all(bf16[256,128,128]{0,2,1:T(8,128)(2,1)} %bitcast.195), channel_id=1, replica_groups=mesh['ctx_0'=4,'ctx_1'=2,'ctx_2'=2,'dp_0'=4,'dp_1'=2] {'ctx_0','ctx_1','..., dimensions={1} | all-to-all | bytes 16777216 | tf_op jit(solution)/shard_map/all_to_all | solution.py:189
  779.5 11.9 %copy.88 = bf16[128,256,128]{2,1,0:T(8,128)(2,1)} copy(bf16[128,256,128]{1,2,0:T(8,128)(2,1)} %bitcast.194) | data formatting | bytes 16777216 | tf_op jit(solution)/shard_map/all_to_all | solution.py:189
  793.5 9.2 fusion.62
  802.7 259.6 %all-gather.8.cloned.1.call-done = bf16[32768,256]{1,0:T(8,128)(2,1)} async-done(((bf16[256,256]{1,0:T(8,128)(2,1)}), bf16[32768,256]{1,0:T(8,128)(2,1)}) %all-gather.8.cloned.1.call-update) | async-done | bytes 16777232 | tf_op jit(solution)/shard_map/all_gather | solution.py:192
  1062.3 10.6 convolution_bitcast_fusion.1
  (292 shorter events, 136.9 us)
Async XLA Ops:
  7.2 352.8 %all-gather.4.cloned.1.call-start = ((), (), s32[]{:S(2)}) async-start(), calls=%async_computation.2 | async-start | bytes 8454144 | tf_op jit(solution)/shard_map/all_gather | solution.py:96
  51.0 318.2 %copy-start.8 = (s32[1,8]{1,0:T(1,128)S(1)}, s32[1,8]{1,0:T(1,128)}, u32[]{:S(2)}) copy-start(s32[1,8]{1,0:T(1,128)} %param.16) | copy-start | bytes 100
  51.0 318.4 %copy-start.5 = (bf16[1,256,1024]{2,1,0:T(8,128)(2,1)S(1)}, bf16[1,256,1024]{2,1,0:T(8,128)(2,1)}, u32[]{:S(2)}) copy-start(bf16[1,256,1024]{2,1,0:T(8,128)(2,1)} %param.12) | copy-start | bytes 1572868
  51.0 318.9 %copy-start.6 = (bf16[1,256,1024]{2,1,0:T(8,128)(2,1)S(1)}, bf16[1,256,1024]{2,1,0:T(8,128)(2,1)}, u32[]{:S(2)}) copy-start(bf16[1,256,1024]{2,1,0:T(8,128)(2,1)} %param.13) | copy-start | bytes 1572868
  51.0 319.9 %copy-start.7 = (s32[1,32]{1,0:T(1,128)S(1)}, s32[1,32]{1,0:T(1,128)}, u32[]{:S(2)}) copy-start(s32[1,32]{1,0:T(1,128)} %param.17) | copy-start | bytes 388
  51.0 368.8 %all-gather.6.cloned.1.call-start = ((), (), s32[]{:S(2)}) async-start(), calls=%async_computation.3 | async-start | bytes 2228224 | tf_op jit(solution)/shard_map/all_gather | solution.py:24
  368.9 283.7 %reduce-scatter.2.cloned.1.call-start = ((), (), s32[]{:S(2)}) async-start(), calls=%async_computation.4 | async-start | bytes 4456448 | tf_op jit(solution)/shard_map/reduce_scatter | solution.py:183
  428.2 62.8 %copy-start = (bf16[1,256,1024]{1,2,0:T(8,128)(2,1)S(1)}, bf16[1,256,1024]{1,2,0:T(8,128)(2,1)}, u32[]{:S(2)}) copy-start(bf16[1,256,1024]{1,2,0:T(8,128)(2,1)} %copy.82) | copy-start | bytes 1572868
  429.9 2.8 copy-start.3
  435.1 1.0 copy-start.4
  437.7 2.8 copy-start.3
  442.9 1.0 copy-start.4
  445.6 2.8 copy-start.3
  453.4 2.8 copy-start.3
  461.3 2.8 copy-start.3
  469.1 2.8 copy-start.3
  474.3 1.0 copy-start.4
  477.0 2.8 copy-start.3
  482.2 1.0 copy-start.4
  484.8 2.8 copy-start.3
  490.0 1.0 copy-start.4
  573.3 489.0 %all-gather.8.cloned.1.call-start = ((), (), s32[]{:S(2)}) async-start(), calls=%async_computation.5 | async-start | bytes 16908288 | tf_op jit(solution)/shard_map/all_gather | solution.py:192
  779.5 12.0 %copy-start.1 = (bf16[256,8,128]{0,2,1:T(8,128)(2,1)S(1)}, bf16[256,8,128]{0,2,1:T(8,128)(2,1)}, u32[]{:S(2)}) copy-start(bf16[256,8,128]{0,2,1:T(8,128)(2,1)} %get-tuple-element.642) | copy-start | bytes 1572868
  779.5 14.0 %copy-start.2 = (bf16[256,256]{1,0:T(8,128)(2,1)S(1)}, bf16[256,256]{1,0:T(8,128)(2,1)}, u32[]{:S(2)}) copy-start(bf16[256,256]{1,0:T(8,128)(2,1)} %convert_element_type.72) | copy-start | bytes 393220
  (3 other events, 2.9 us)
Sparse Core Ops, SparseCore 0:
  51.1 308.8 all-gather.3
  369.0 50.7 all-gather.5
  573.4 79.1 reduce-scatter.1
  654.3 407.9 all-gather.7
where the time goes:
time: 1090 us; the launch traced here: 1080 us
  waiting for transfers between devices  697 us (64%)
  blocking collectives  152 us (14%)
  matrix products  119 us (11%)
  local copies, waits for them, and re-layouts  62.4 us (6%)
  other arithmetic  23.8 us (2%)
  between operations  15.3 us (1%)
  loops' own time  11.6 us (1%)
    all_gather x1, waiting for transfers between devices, body(): both = lax.all_gather(local_rows, CTX_DP, axis=0, tiled=True)  309 us
    all_gather x1, waiting for transfers between devices, body(): lax.all_gather(grads_kv, CTX_DP, axis=0, tiled=True)  260 us
    all_to_all x1, blocking collectives, body(): lax.all_to_all(token_rows, CTX_DP, split_axis=1, concat_axis=0, tiled=True)  113 us
    reduce_scatter x1, waiting for transfers between devices, body(): lax.psum_scatter(key_terms, CTX, scatter_dimension=0, tiled=True)  79.2 us
    all_gather x1, waiting for transfers between devices, in_one_piece(): result, at, done = (lax.all_gather(both, axis, axis=dim, tiled=True), 0, [])  48.8 us
    psum x5, blocking collectives, over_axes(): value = lax.psum(value, axis)  38.6 us
  transfers between devices with their start and end apart: 4, of which 4 were waited for; matrix products, arithmetic and copies ran while one was open for 3% of the time, Pallas kernels for 0%

commit v1 on v0

v1 whole, which is shorter than its diff:
```python
import functools

import jax
import jax.numpy as jnp
import numpy as np
from jax import lax
from jax.experimental import pallas as pl
from jax.experimental.pallas import tpu as pltpu
from jax.sharding import Mesh
from jax.sharding import PartitionSpec as P

AXES = ("y", "zh", "core", "x", "zl")
SIZES = (4, 2, 2, 4, 2)
CTX = ("y", "zh", "core")
DP = ("x", "zl")
SAME_CORE_CTX = ("y", "zh")
DEVICES = int(np.prod(SIZES))

EPSILON = 1e-05
NEGATIVE = -1e30
KEY_CHUNK = 256

RING_ORDER = {0: ("x", "y", "z"), 1: ("y", "z", "x")}
OFFSETS = (0, -1, 1, 2)


def coordinates(device):
    y, zh, core, x, zl = (int(v) for v in np.unravel_index(device, SIZES))
    return {"y": y, "z": zh * 2 + zl, "x": x, "core": core}


def device_of(place):
    return int(
        np.ravel_multi_index(
            (place["y"], place["z"] // 2, place["core"], place["x"], place["z"] % 2), SIZES
        )
    )


def moved(change):
    pairs = []
    for device in range(DEVICES):
        place = coordinates(device)
        change(place)
        pairs.append((device, device_of(place)))
    return pairs


def along_ring(phase, step):
    def change(place):
        axis = RING_ORDER[place["core"]][phase]
        place[axis] = (place[axis] + step) % 4

    return moved(change)


def to_other_core(place):
    place["core"] = 1 - place["core"]


def swap_cores(value):
    return lax.ppermute(value, AXES, moved(to_other_core))


def block_table():
    table = np.zeros((DEVICES, DEVICES), np.int32)
    for device in range(DEVICES):
        here = coordinates(device)
        at = 0
        for core in (here["core"], 1 - here["core"]):
            order = RING_ORDER[core]
            for last in OFFSETS:
                for middle in OFFSETS:
                    for first in OFFSETS:
                        place = dict(here, core=core)
                        for axis, step in zip(order, (first, middle, last)):
                            place[axis] = (place[axis] + step) % 4
                        table[device, at] = device_of(place)
                        at += 1
    return table


def gather_ring(value, phase):
    return [value] + [
        lax.ppermute(value, AXES, along_ring(phase, -offset)) for offset in OFFSETS[1:]
    ]


def reduce_ring(pieces, phase):
    total = pieces[0]
    for piece, offset in zip(pieces[1:], OFFSETS[1:]):
        sent = lax.ppermute(piece.astype(jnp.bfloat16), AXES, along_ring(phase, offset))
        total = total + sent.astype(jnp.float32)
    return total


def levels(ratio):
    return jnp.where(ratio >= 0.5, 1.0, jnp.where(ratio <= -0.5, -1.0, 0.0)).astype(jnp.float32)


def shuffle_kernel(table, tokens, own, other, own_sem, other_sem):
    width = own.shape[1] * 2 // DEVICES
    for half, (out, sem) in enumerate(((other, other_sem), (own, own_sem))):
        first = 0 if half else DEVICES // 2

        def start(j, _, out=out, sem=sem, first=first):
            source = pl.ds(pl.multiple_of(table[first + j] * width, width), width)
            target = pl.ds(pl.multiple_of(j * width, width), width)
            pltpu.make_async_copy(tokens.at[:, source], out.at[:, target], sem).start()
            return 0

        lax.fori_loop(0, DEVICES // 2, start, 0)
    pltpu.make_async_copy(other, other, other_sem).wait()
    pltpu.make_async_copy(own, own, own_sem).wait()


def shuffle(table, tokens):
    rows, features = tokens.shape
    half = jax.ShapeDtypeStruct((rows, features // 2), tokens.dtype)
    anywhere = pl.BlockSpec(memory_space=pl.ANY)
    return pl.pallas_call(
        shuffle_kernel,
        out_shape=(half, half),
        in_specs=[pl.BlockSpec(memory_space=pltpu.SMEM), anywhere],
        out_specs=(anywhere, anywhere),
        scratch_shapes=[pltpu.SemaphoreType.DMA, pltpu.SemaphoreType.DMA],
        cost_estimate=pl.CostEstimate(
            flops=0, bytes_accessed=4 * rows * features, transcendentals=0
        ),
        name="shuffle_tokens",
    )(table, tokens)


def token_grad_kernel(table, grads, *rest, count):
    weights, out = rest[:count], rest[count]
    buffers, sems = rest[count + 1 :]
    rows, step_width = buffers.shape[1:]
    width = out.shape[1] // DEVICES
    per_step = step_width // width
    steps_each = weights[0].shape[0] // step_width
    for step in range(count * steps_each):
        slot = step % 2
        buffer, sem = buffers.at[slot], sems.at[slot]
        if step >= 2:
            pltpu.make_async_copy(buffer, buffer, sem).wait()
        part = (step % steps_each) * step_width
        buffers[slot] = lax.dot_general(
            grads[...],
            weights[step // steps_each][part : part + step_width, :],
            (((1,), (1,)), ((), ())),
            preferred_element_type=jnp.float32,
        ).astype(jnp.bfloat16)
        for j in range(per_step):
            target = pl.ds(pl.multiple_of(table[step * per_step + j] * width, width), width)
            pltpu.make_async_copy(
                buffer.at[:, j * width : (j + 1) * width], out.at[:, target], sem
            ).start()
    for slot in range(2):
        pltpu.make_async_copy(buffers.at[slot], buffers.at[slot], sems.at[slot]).wait()


def token_gradient(table, grads, weights):
    rows, both = grads.shape
    features = sum(w.shape[0] for w in weights)
    step_width = 1024
    in_vmem = pl.BlockSpec(memory_space=pltpu.VMEM)
    return pl.pallas_call(
        functools.partial(token_grad_kernel, count=len(weights)),
        out_shape=jax.ShapeDtypeStruct((rows, features), jnp.bfloat16),
        in_specs=[pl.BlockSpec(memory_space=pltpu.SMEM)] + [in_vmem] * (1 + len(weights)),
        out_specs=pl.BlockSpec(memory_space=pl.ANY),
        scratch_shapes=[
            pltpu.VMEM((2, rows, step_width), jnp.bfloat16),
            pltpu.SemaphoreType.DMA((2,)),
        ],
        compiler_params=pltpu.CompilerParams(vmem_limit_bytes=32 << 20),
        cost_estimate=pl.CostEstimate(
            flops=2 * rows * both * features,
            bytes_accessed=2 * features * (rows + both),
            transcendentals=0,
        ),
        name="token_gradient",
    )(table, grads, *weights)


def attention_kernel(
    meta, queries, cotangent, kv_same, kv_other, mixed_out, query_grad, same_out, other_out,
    keys, values, key_acc, value_acc, scores, q_columns, c_columns, q_rows, c_rows,
    *, heads, head_size, block, docs, blocks,
):
    scale = head_size ** (-0.5)
    columns = heads * block
    ctx, core = meta[docs + blocks], meta[docs + blocks + 1]
    sides = ((kv_same, core, same_out), (kv_other, 1 - core, other_out))

    def rows_at(index, size):
        return pl.ds(pl.multiple_of(index * size, size), size)

    def true_block(core_of, j):
        return meta[docs + ((j // 2) * 2 + core_of) * 2 + j % 2]

    for ref, core_of, _ in sides:
        for j in range(blocks // 2):
            target = rows_at(true_block(core_of, j), block)
            keys[target, :] = ref[j * block : (j + 1) * block, :head_size]
            values[target, :] = ref[j * block : (j + 1) * block, head_size:]
    key_acc[...] = jnp.zeros_like(key_acc)
    value_acc[...] = jnp.zeros_like(value_acc)

    def one_block(i, _):
        here = rows_at(i, block)
        for h in range(heads):
            head = slice(h * head_size, (h + 1) * head_size)
            part = slice(h * block, (h + 1) * block)
            q, c = queries[here, head], cotangent[here, head]
            q_rows[part, :], c_rows[part, :] = q, c
            q_columns[:, part], c_columns[:, part] = q.T, c.T
        start = meta[docs + 2 * ctx + i] * block
        position = start + lax.rem(lax.broadcasted_iota(jnp.int32, (1, columns), 1), block)
        own_start = jnp.zeros((1, columns), jnp.int32)
        first = jnp.int32(0)
        for d in range(docs):
            doc_start = meta[d]
            own_start = jnp.maximum(own_start, jnp.where(position >= doc_start, doc_start, 0))
            first = jnp.maximum(first, jnp.where(start >= doc_start, doc_start, 0))
        lowest = first // KEY_CHUNK
        count = (start + block - 1) // KEY_CHUNK - lowest + 1

        def score(c, best):
            s = scale * jnp.dot(
                keys[rows_at(lowest + c, KEY_CHUNK), :],
                q_columns[...],
                preferred_element_type=jnp.float32,
            )
            key_pos = (lowest + c) * KEY_CHUNK + lax.broadcasted_iota(
                jnp.int32, (KEY_CHUNK, columns), 0
            )
            s = jnp.where((key_pos >= own_start) & (key_pos <= position), s, NEGATIVE)
            scores[c] = s
            return jnp.maximum(best, jnp.max(s.reshape(KEY_CHUNK // 8, 8, columns), axis=0))

        best = lax.fori_loop(
            0, count, score, jnp.full((8, columns), NEGATIVE, jnp.float32)
        )
        best = jnp.max(best, axis=0, keepdims=True)

        def mix(c, carried):
            total, acc = carried
            w = jnp.exp(scores[c] - best)
            scores[c] = w
            total = total + jnp.sum(w.reshape(KEY_CHUNK // 8, 8, columns), axis=0)
            acc = acc + lax.dot_general(
                values[rows_at(lowest + c, KEY_CHUNK), :],
                w.astype(jnp.bfloat16),
                (((0,), (0,)), ((), ())),
                preferred_element_type=jnp.float32,
            )
            return total, acc

        total, acc = lax.fori_loop(
            0,
            count,
            mix,
            (jnp.zeros((8, columns), jnp.float32), jnp.zeros((head_size, columns), jnp.float32)),
        )
        total = jnp.sum(total, axis=0, keepdims=True)
        mixed = (acc / total).astype(jnp.bfloat16)
        expected = jnp.sum(
            mixed.astype(jnp.float32) * c_columns[...].astype(jnp.float32), axis=0, keepdims=True
        )
        per_total = 1.0 / total
        for h in range(heads):
            mixed_out[here, h * head_size : (h + 1) * head_size] = mixed[
                :, h * block : (h + 1) * block
            ].T

        def back(c, q_acc):
            at = rows_at(lowest + c, KEY_CHUNK)
            probability = scores[c] * per_total
            prob_grad = jnp.dot(values[at, :], c_columns[...], preferred_element_type=jnp.float32)
            score_grad = (probability * (prob_grad - expected)).astype(jnp.bfloat16)
            key_acc[at, :] += jnp.dot(score_grad, q_rows[...], preferred_element_type=jnp.float32)
            value_acc[at, :] += jnp.dot(
                probability.astype(jnp.bfloat16), c_rows[...], preferred_element_type=jnp.float32
            )
            return q_acc + lax.dot_general(
                keys[at, :],
                score_grad,
                (((0,), (0,)), ((), ())),
                preferred_element_type=jnp.float32,
            )

        q_acc = lax.fori_loop(
            0, count, back, jnp.zeros((head_size, columns), jnp.float32)
        )
        q_grad = (q_acc * scale).astype(jnp.bfloat16)
        for h in range(heads):
            query_grad[here, h * head_size : (h + 1) * head_size] = q_grad[
                :, h * block : (h + 1) * block
            ].T
        return 0

    lax.fori_loop(0, queries.shape[0] // block, one_block, 0)
    for _, core_of, out in sides:
        for j in range(blocks // 2):
            source = rows_at(true_block(core_of, j), block)
            part = slice(j * block, (j + 1) * block)
            out[part, :head_size] = (key_acc[source, :] * scale).astype(out.dtype)
            out[part, head_size:] = value_acc[source, :].astype(out.dtype)


def attention(meta, queries, cotangent, kv_same, kv_other, head_size, docs, blocks):
    rows, width = queries.shape
    heads = width // head_size
    length = kv_same.shape[0] + kv_other.shape[0]
    block = length // blocks
    columns = heads * block
    in_vmem = pl.BlockSpec(memory_space=pltpu.VMEM)
    most_chunks = 10
    visible = 9 * KEY_CHUNK
    return pl.pallas_call(
        functools.partial(
            attention_kernel, heads=heads, head_size=head_size, block=block, docs=docs, blocks=blocks
        ),
        out_shape=(
            jax.ShapeDtypeStruct((rows, width), jnp.bfloat16),
            jax.ShapeDtypeStruct((rows, width), jnp.bfloat16),
            jax.ShapeDtypeStruct(kv_same.shape, jnp.float32),
            jax.ShapeDtypeStruct(kv_other.shape, jnp.bfloat16),
        ),
        in_specs=[pl.BlockSpec(memory_space=pltpu.SMEM)] + [in_vmem] * 4,
        out_specs=(in_vmem,) * 4,
        scratch_shapes=[
            pltpu.VMEM((length, head_size), jnp.bfloat16),
            pltpu.VMEM((length, head_size), jnp.bfloat16),
            pltpu.VMEM((length, head_size), jnp.float32),
            pltpu.VMEM((length, head_size), jnp.float32),
            pltpu.VMEM((most_chunks, KEY_CHUNK, columns), jnp.float32),
            pltpu.VMEM((head_size, columns), jnp.bfloat16),
            pltpu.VMEM((head_size, columns), jnp.bfloat16),
            pltpu.VMEM((columns, head_size), jnp.bfloat16),
            pltpu.VMEM((columns, head_size), jnp.bfloat16),
        ],
        compiler_params=pltpu.CompilerParams(vmem_limit_bytes=40 << 20),
        cost_estimate=pl.CostEstimate(
            flops=14 * rows * heads * visible * head_size,
            bytes_accessed=8 * rows * width + 8 * length * head_size,
            transcendentals=rows * heads * visible,
        ),
        name="masked_attention",
    )(meta, queries, cotangent, kv_same, kv_other)


def exchange_sums(row):
    tile = jnp.broadcast_to(row[None], (DEVICES, 8, row.shape[1])).reshape(-1, row.shape[1])
    everyones = lax.all_to_all(tile, AXES, split_axis=0, concat_axis=0, tiled=True)
    return jnp.sum(everyones.reshape(DEVICES, 8, row.shape[1]), axis=0)[:1]


def body(tokens, queries, cotangent, latent_key, latent_value, lengths, block_order):
    token_rows = tokens[0]
    rows_here, features = token_rows.shape
    head_size = latent_key.shape[1]
    docs, blocks = lengths.shape[1], block_order.shape[1]
    me = lax.axis_index(AXES)
    table = lax.dynamic_index_in_dim(jnp.asarray(block_table()), me, keepdims=False)
    before = np.arange(docs)[:, None] < np.arange(docs)[None, :]
    doc_starts = jnp.sum(jnp.where(before, lengths[0][:, None], 0), axis=0)
    meta = jnp.concatenate(
        [
            doc_starts.astype(jnp.int32),
            block_order[0],
            jnp.stack([lax.axis_index(CTX), lax.axis_index("core")]).astype(jnp.int32),
        ]
    )

    lane = lax.broadcasted_iota(jnp.int32, (1, 128), 1)
    sums = exchange_sums(
        jnp.where(
            lane == 0,
            jnp.sum(jnp.abs(latent_key)),
            jnp.where(lane == 1, jnp.sum(jnp.abs(latent_value)), 0.0),
        )
    )
    entry_count = features * head_size
    key_scale = sums[0, 0] / entry_count + EPSILON
    value_scale = sums[0, 1] / entry_count + EPSILON
    weights = jnp.concatenate(
        [
            (key_scale * levels(latent_key / key_scale)).astype(jnp.bfloat16),
            (value_scale * levels(latent_value / value_scale)).astype(jnp.bfloat16),
        ],
        axis=1,
    )

    tokens_own, tokens_other = shuffle(table, token_rows)
    tokens_peer = swap_cores(tokens_other)
    for phase in range(2):
        weights = jnp.concatenate(gather_ring(weights, phase), axis=0)
    weight_parts = gather_ring(weights, 2)
    part_rows = weights.shape[0]

    def project(rows):
        total = 0.0
        for i, part in enumerate(weight_parts):
            total = total + jnp.dot(
                rows[:, i * part_rows : (i + 1) * part_rows],
                part,
                preferred_element_type=jnp.float32,
            )
        return total

    peers_share = swap_cores(project(tokens_peer))
    kv_here = (project(tokens_own) + peers_share).astype(jnp.bfloat16)
    groups = lax.axis_size(SAME_CORE_CTX)
    kv_same = lax.all_to_all(
        jnp.broadcast_to(kv_here[None], (groups,) + kv_here.shape).reshape(-1, 2 * head_size),
        SAME_CORE_CTX,
        split_axis=0,
        concat_axis=0,
        tiled=True,
    )
    kv_other = swap_cores(kv_same)
    other_parts = [swap_cores(part) for part in weight_parts]

    mixed, query_grad, same_terms, other_terms = attention(
        meta, queries[0], cotangent[0], kv_same, kv_other, head_size, docs, blocks
    )
    chip_terms = (same_terms + swap_cores(other_terms).astype(jnp.float32)).astype(jnp.bfloat16)
    terms = lax.all_to_all(chip_terms, SAME_CORE_CTX, split_axis=0, concat_axis=0, tiled=True)
    grads = jnp.sum(
        terms.reshape(groups, rows_here, 2 * head_size).astype(jnp.float32), axis=0
    ).astype(jnp.bfloat16)
    peer_grads = swap_cores(grads)

    def weight_term(i):
        cut = slice(i * part_rows, (i + 1) * part_rows)
        return sum(
            lax.dot_general(
                rows[:, cut], g, (((0,), (0,)), ((), ())), preferred_element_type=jnp.float32
            )
            for rows, g in ((tokens_own, grads), (tokens_peer, peer_grads))
        )

    summed = reduce_ring([weight_term(i) for i in range(4)], 2)
    token_grad = token_gradient(table, grads, weight_parts + other_parts)
    for phase in (1, 0):
        summed = reduce_ring(jnp.split(summed, 4, axis=0), phase)
    return (
        mixed[None],
        query_grad[None],
        token_grad[None],
        summed[:, :head_size],
        summed[:, head_size:],
    )


def solution(mesh):
    torus = Mesh(mesh.devices.reshape(SIZES), AXES)
    whole = CTX + DP
    in_specs = (
        P(DP, CTX, None),
        P(DP, CTX, None),
        P(DP, CTX, None),
        P(whole, None),
        P(whole, None),
        P(DP, None),
        P(DP, None),
    )
    out_specs = (
        P(DP, CTX, None),
        P(DP, CTX, None),
        P(DP, CTX, None),
        P(whole, None),
        P(whole, None),
    )
    return jax.shard_map(body, mesh=torus, in_specs=in_specs, out_specs=out_specs, check_vma=False)
```

time: 1090 us -> 500 us (0.46)
  waiting for transfers between devices: 697 us -> 83.8 us
  Pallas kernels: 0 us -> 280 us
  matrix products: 119 us -> 21.9 us
  blocking collectives: 152 us -> 77.4 us
  local copies, waits for them, and re-layouts: 62.4 us -> 4.85 us
  starting transfers between devices: 0.34 us -> 25.5 us
  other arithmetic: 23.8 us -> 4.16 us
  between operations: 15.3 us -> 2.7 us
  loops' own time: 11.6 us -> 0 us
    all_gather x3 -> x0, waiting for transfers between devices: 617 us -> none  [the longest x1 309 us: body(): both = lax.all_gather(local_rows, CTX_DP, axis=0, tiled=True)]
    pallas_call x0 -> x3, Pallas kernels: none -> 280 us  [the longest x1 256 us: shuffle(): pl.pallas_call(shuffle_kernel, out_shape=(half, half), in_specs=[pl.Block...]
    dot_general x59 -> x16, matrix products: 119 us -> 21.9 us  [the longest x8 11.9 us: weight_term(): lax.dot_general(rows[:, cut], g, (((0,), (0,)), ((), ())), preferred_elem...]
    ppermute x0 -> x27, waiting for transfers between devices: none -> 83.8 us  [the longest x9 43 us: reduce_ring(): lax.ppermute(piece.astype(jnp.bfloat16), AXES, along_ring(phase, offset))]
    reduce_scatter x1 -> x0, waiting for transfers between devices: 79.2 us -> none  [body(): lax.psum_scatter(key_terms, CTX, scatter_dimension=0, tiled=True)]
    psum x5 -> x0, blocking collectives: 38.6 us -> none  [over_axes(): value = lax.psum(value, axis)]
    all_to_all x1 -> x3, blocking collectives: 113 us -> 77.4 us  [the longest x1 29.6 us: body(): lax.all_to_all(chip_terms, SAME_CORE_CTX, split_axis=0, concat_axis=0, ti...]
    ppermute x0 -> x27, starting transfers between devices: none -> 25.5 us  [the longest x9 14.1 us: reduce_ring(): lax.ppermute(piece.astype(jnp.bfloat16), AXES, along_ring(phase, offset))]
  transfers between devices with their start and end apart: 4 -> 27, of which waited for: 4 -> 16; matrix products, arithmetic and copies ran while one was open for 3% -> 3% of each run, Pallas kernels for 0% -> 2%
where the time goes in v1:
time: 500 us
  Pallas kernels  280 us (56%)
  waiting for transfers between devices  83.8 us (17%)
  blocking collectives  77.4 us (15%)
  starting transfers between devices  25.5 us (5%)
  matrix products  21.9 us (4%)
    pallas_call x1, Pallas kernels, shuffle(): pl.pallas_call(shuffle_kernel, out_shape=(half, half), in_specs=[pl.Block...  256 us
    ppermute x9, waiting for transfers between devices, reduce_ring(): lax.ppermute(piece.astype(jnp.bfloat16), AXES, along_ring(phase, offset))  43 us
    ppermute x9, waiting for transfers between devices, gather_ring(): lax.ppermute(value, AXES, along_ring(phase, -offset))  34.2 us
    all_to_all x1, blocking collectives, body(): lax.all_to_all(chip_terms, SAME_CORE_CTX, split_axis=0, concat_axis=0, ti...  29.6 us
    all_to_all x1, blocking collectives, exchange_sums(): lax.all_to_all(tile, AXES, split_axis=0, concat_axis=0, tiled=True)  24.2 us
    all_to_all x1, blocking collectives, body(): lax.all_to_all(jnp.broadcast_to(kv_here[None], (groups,) + kv_here.shape)...  23.5 us
    ppermute x9, starting transfers between devices, reduce_ring(): lax.ppermute(piece.astype(jnp.bfloat16), AXES, along_ring(phase, offset))  14.1 us
    pallas_call x1, Pallas kernels, attention(): pl.pallas_call(functools.partial(attention_kernel, heads=heads, head_size...  13.8 us
  transfers between devices with their start and end apart: 27, of which 16 were waited for; matrix products, arithmetic and copies ran while one was open for 3% of the time, Pallas kernels for 2%

profile of v1, /device:TPU:0, one launch (start us, length us, event | category | flops | bytes accessed | tf_op | source)
XLA Modules:
  0.0 499.8 jit_solution(16984428007507440270)
XLA Ops:
  1.9 256.0 %shuffle_tokens.1 = (bf16[256,8192]{1,0:T(8,128)(2,1)}, bf16[256,8192]{1,0:T(8,128)(2,1)}) custom-call(s32[128]{0:T(128)} %dynamic-slice_bitcast_fusion.table, bf16[256,16384]{1,0:T(8,128)(2,1)} %bitcast.35), custom_call_target="tpu_custom_call" | custom-call | bytes 16777216 | tf_op jit(solution)/shard_map/shuffle_tokens/pallas_call | solution.py:121
  260.0 24.2 %all_to_all.23 = f32[128,8,128]{2,1,0:T(8,128)S(1)} all-to-all(f32[128,8,128]{2,1,0:T(8,128)S(1)} %reshape.54), channel_id=1, replica_groups=mesh['y'=4,'zh'=2,'core'=2,'x'=4,'zl'=2] {'y','zh','core','x','zl'}, dimensions={0} | all-to-all | bytes 1048576 | tf_op jit(solution)/shard_map/all_to_all | solution.py:356
  287.2 2.8 collective-permute-start.1
  289.9 2.2 collective-permute-done
  292.5 3.3 collective-permute-done.2
  296.4 2.6 collective-permute-start.4
  299.1 4.3 collective-permute-done.3
  303.4 2.4 collective-permute-done.4
  308.2 2.2 collective-permute-start.7
  310.4 13.0 %collective-permute-done.8.rest_3_ = bf16[2048,256]{1,0:T(8,128)(2,1)S(1)} collective-permute-done((bf16[2048,256]{1,0:T(8,128)(2,1)S(1)}, bf16[2048,256]{1,0:T(8,128)(2,1)S(1)}, u32[]{:S(2)}, u32[]{:S(2)}) %collective-permute-start.8) | collective-permute-done | bytes 1048608 | tf_op jit(solution)/shard_map/ppermute | solution.py:85
  325.1 7.7 %collective-permute-done.7.rest_2_ = bf16[2048,256]{1,0:T(8,128)(2,1)S(1)} collective-permute-done((bf16[2048,256]{1,0:T(8,128)(2,1)S(1)}, bf16[2048,256]{1,0:T(8,128)(2,1)S(1)}, u32[]{:S(2)}, u32[]{:S(2)}) %collective-permute-start.7) | collective-permute-done | bytes 1048608 | tf_op jit(solution)/shard_map/ppermute | solution.py:85
  342.5 23.5 %all_to_all.24 = bf16[8,256,256]{2,1,0:T(8,128)(2,1)} all-to-all(bf16[8,256,256]{2,1,0:T(8,128)(2,1)S(1)} %broadcast_in_dim.69), channel_id=1, replica_groups=mesh['y'=4,'zh'=2,'core'=2,'x'=4,'zl'=2] {'y','zh'}, dimensions={0} | all-to-all | bytes 2097152 | tf_op jit(solution)/shard_map/all_to_all | solution.py:416
  366.2 2.8 collective-permute-done.11.kv_other
  371.1 13.8 %masked_attention.1 = (bf16[256,1024]{1,0:T(8,128)(2,1)}, bf16[256,1024]{1,0:T(8,128)(2,1)}, f32[2048,256]{1,0:T(8,128)S(1)}, bf16[2048,256]{1,0:T(8,128)(2,1)S(1)}) custom-call(s32[42]{0:T(128)S(1)} %pad_add_fusion.meta, bf16[256,1024]{1,0:T(8,128)(2,1)S(1)} %bitcast.32, bf16[256,1024]{1,0:T(8,128)(2,1)S(1)} %bitcast.33, ...), custom_call_target="tpu_custom_call" | custom-call | flops 8455716864 | bytes 6291456 | tf_op jit(solution)/shard_map/masked_attention/pallas_call | solution.py:321
  384.8 2.7 collective-permute-done.12
  387.8 29.6 %all_to_all.25 = bf16[8,256,256]{2,1,0:T(8,128)(2,1)} all-to-all(bf16[8,256,256]{2,1,0:T(8,128)(2,1)S(1)} %bitcast.36), channel_id=1, replica_groups=mesh['y'=4,'zh'=2,'core'=2,'x'=4,'zl'=2] {'y','zh'}, dimensions={0} | all-to-all | bytes 2097152 | tf_op jit(solution)/shard_map/all_to_all | solution.py:430
  424.8 5.6 %collective-permute-start.18 = (bf16[2048,256]{1,0:T(8,128)(2,1)S(1)}, bf16[2048,256]{1,0:T(8,128)(2,1)S(1)}, u32[]{:S(2)}, u32[]{:S(2)}) collective-permute-start(bf16[2048,256]{1,0:T(8,128)(2,1)S(1)} %fusion.3), channel_id=1, source_target_pairs={{0,17},{1,0},{2,19},{3,2},{4,21},{5,4},{6,23},{7,6},{8,14},{9,15},... | collective-permute-start | bytes 3145736 | tf_op jit(solution)/shard_map/ppermute | solution.py:92
  436.3 17.7 %collective-permute-done.18 = bf16[2048,256]{1,0:T(8,128)(2,1)S(1)} collective-permute-done((bf16[2048,256]{1,0:T(8,128)(2,1)S(1)}, bf16[2048,256]{1,0:T(8,128)(2,1)S(1)}, u32[]{:S(2)}, u32[]{:S(2)}) %collective-permute-start.18) | collective-permute-done | bytes 1048608 | tf_op jit(solution)/shard_map/ppermute | solution.py:92
  454.0 5.5 %collective-permute-done.19 = bf16[2048,256]{1,0:T(8,128)(2,1)S(1)} collective-permute-done((bf16[2048,256]{1,0:T(8,128)(2,1)S(1)}, bf16[2048,256]{1,0:T(8,128)(2,1)S(1)}, u32[]{:S(2)}, u32[]{:S(2)}) %collective-permute-start.19) | collective-permute-done | bytes 1048608 | tf_op jit(solution)/shard_map/ppermute | solution.py:92
  464.0 4.2 collective-permute-done.21
  468.7 7.0 %collective-permute-done.22 = bf16[512,256]{1,0:T(8,128)(2,1)S(1)} collective-permute-done((bf16[512,256]{1,0:T(8,128)(2,1)S(1)}, bf16[512,256]{1,0:T(8,128)(2,1)S(1)}, u32[]{:S(2)}, u32[]{:S(2)}) %collective-permute-start.22) | collective-permute-done | bytes 262176 | tf_op jit(solution)/shard_map/ppermute | solution.py:92
  475.9 8.6 %collective-permute-done.23 = bf16[512,256]{1,0:T(8,128)(2,1)S(1)} collective-permute-done((bf16[512,256]{1,0:T(8,128)(2,1)S(1)}, bf16[512,256]{1,0:T(8,128)(2,1)S(1)}, u32[]{:S(2)}, u32[]{:S(2)}) %collective-permute-start.23) | collective-permute-done | bytes 262176 | tf_op jit(solution)/shard_map/ppermute | solution.py:92
  486.8 2.5 collective-permute-start.26
  489.3 9.8 %token_gradient.1 = bf16[256,16384]{1,0:T(8,128)(2,1)} custom-call(s32[128]{0:T(128)S(1)} %copy-done.2, bf16[256,256]{1,0:T(8,128)(2,1)S(1)} %reduce_sum.52.grads, bf16[2048,256]{1,0:T(8,128)(2,1)S(1)} %constant_dynamic-update-slice_fusion.rest_0_, bf16[2048,256]{1,0:T(8,128)(2,1)S(1)} %copy-done.1, bf16[2048,256]{1,0:T(8,128)(2,1)S(1)} %collective-permute-done.7.rest_2_, ...), custom_call_target="tpu_custom_call" | custom-call | flops 2147483648 | bytes 16777216 | tf_op jit(solution)/shard_map/token_gradient/pallas_call | solution.py:167
  (102 shorter events, 43.2 us)
Async XLA Ops:
  257.9 75.3 %collective-permute-start.9 = (bf16[256,8192]{1,0:T(8,128)(2,1)}, bf16[256,8192]{1,0:T(8,128)(2,1)}, u32[]{:S(2)}, u32[]{:S(2)}) collective-permute-start(bf16[256,8192]{1,0:T(8,128)(2,1)} %get-tuple-element.12), channel_id=1, source_target_pairs={{0,8},{1,9},{2,10},{3,11},{4,12},{5,13},{6,14},{7,15},{8,0},{9,1},... | collective-permute-start | bytes 12582920 | tf_op jit(solution)/shard_map/ppermute | solution.py:62
  286.6 5.5 %collective-permute-start = (bf16[128,256]{1,0:T(8,128)(2,1)S(1)}, bf16[128,256]{1,0:T(8,128)(2,1)S(1)}, u32[]{:S(2)}, u32[]{:S(2)}) collective-permute-start(bf16[128,256]{1,0:T(8,128)(2,1)S(1)} %get-tuple-element.27), channel_id=1, source_target_pairs={{0,2},{1,3},{2,4},{3,5},{4,6},{5,7},{6,0},{7,1},{8,40},{9,41},{10,... | collective-permute-start | bytes 196616 | tf_op jit(solution)/shard_map/ppermute | solution.py:85
  287.2 5.3 %collective-permute-start.1 = (bf16[128,256]{1,0:T(8,128)(2,1)S(1)}, bf16[128,256]{1,0:T(8,128)(2,1)S(1)}, u32[]{:S(2)}, u32[]{:S(2)}) collective-permute-start(bf16[128,256]{1,0:T(8,128)(2,1)S(1)} %get-tuple-element.27), channel_id=1, source_target_pairs={{0,6},{1,7},{2,0},{3,1},{4,2},{5,3},{6,4},{7,5},{8,104},{9,105},{1... | collective-permute-start | bytes 196616 | tf_op jit(solution)/shard_map/ppermute | solution.py:85
  289.9 5.8 %collective-permute-start.2 = (bf16[128,256]{1,0:T(8,128)(2,1)S(1)}, bf16[128,256]{1,0:T(8,128)(2,1)S(1)}, u32[]{:S(2)}, u32[]{:S(2)}) collective-permute-start(bf16[128,256]{1,0:T(8,128)(2,1)S(1)} %get-tuple-element.27), channel_id=1, source_target_pairs={{0,4},{1,5},{2,6},{3,7},{4,0},{5,1},{6,2},{7,3},{8,72},{9,73},{10,... | collective-permute-start | bytes 196616 | tf_op jit(solution)/shard_map/ppermute | solution.py:85
  295.7 7.7 %collective-permute-start.3 = (bf16[512,256]{1,0:T(8,128)(2,1)S(1)}, bf16[512,256]{1,0:T(8,128)(2,1)S(1)}, u32[]{:S(2)}, u32[]{:S(2)}) collective-permute-start(bf16[512,256]{1,0:T(8,128)(2,1)S(1)} %pad_maximum_fusion), channel_id=1, source_target_pairs={{0,32},{1,33},{2,34},{3,35},{4,36},{5,37},{6,38},{7,39},{8,9},{9,2... | collective-permute-start | bytes 786440 | tf_op jit(solution)/shard_map/ppermute | solution.py:85
  296.4 9.3 %collective-permute-start.4 = (bf16[512,256]{1,0:T(8,128)(2,1)S(1)}, bf16[512,256]{1,0:T(8,128)(2,1)S(1)}, u32[]{:S(2)}, u32[]{:S(2)}) collective-permute-start(bf16[512,256]{1,0:T(8,128)(2,1)S(1)} %pad_maximum_fusion), channel_id=1, source_target_pairs={{0,96},{1,97},{2,98},{3,99},{4,100},{5,101},{6,102},{7,103},{8,25}... | collective-permute-start | bytes 786440 | tf_op jit(solution)/shard_map/ppermute | solution.py:85
  299.0 7.9 %collective-permute-start.5 = (bf16[512,256]{1,0:T(8,128)(2,1)S(1)}, bf16[512,256]{1,0:T(8,128)(2,1)S(1)}, u32[]{:S(2)}, u32[]{:S(2)}) collective-permute-start(bf16[512,256]{1,0:T(8,128)(2,1)S(1)} %pad_maximum_fusion), channel_id=1, source_target_pairs={{0,64},{1,65},{2,66},{3,67},{4,68},{5,69},{6,70},{7,71},{8,24},{9,... | collective-permute-start | bytes 786440 | tf_op jit(solution)/shard_map/ppermute | solution.py:85
  306.9 16.5 %collective-permute-start.8 = (bf16[2048,256]{1,0:T(8,128)(2,1)S(1)}, bf16[2048,256]{1,0:T(8,128)(2,1)S(1)}, u32[]{:S(2)}, u32[]{:S(2)}) collective-permute-start(bf16[2048,256]{1,0:T(8,128)(2,1)S(1)} %constant_dynamic-update-slice_fusion.rest_0_), channel_id=1, source_target_pairs={{0,16},{1,17},{2,18},{3,19},{4,20},{5,21},{6,22},{7,23},{8,12},{9,... | collective-permute-start | bytes 3145736 | tf_op jit(solution)/shard_map/ppermute | solution.py:85
  308.2 24.5 %collective-permute-start.7 = (bf16[2048,256]{1,0:T(8,128)(2,1)S(1)}, bf16[2048,256]{1,0:T(8,128)(2,1)S(1)}, u32[]{:S(2)}, u32[]{:S(2)}) collective-permute-start(bf16[2048,256]{1,0:T(8,128)(2,1)S(1)} %constant_dynamic-update-slice_fusion.rest_0_), channel_id=1, source_target_pairs={{0,17},{1,0},{2,19},{3,2},{4,21},{5,4},{6,23},{7,6},{8,14},{9,15},... | collective-permute-start | bytes 3145736 | tf_op jit(solution)/shard_map/ppermute | solution.py:85
  310.4 26.1 %collective-permute-start.6 = (bf16[2048,256]{1,0:T(8,128)(2,1)S(1)}, bf16[2048,256]{1,0:T(8,128)(2,1)S(1)}, u32[]{:S(2)}, u32[]{:S(2)}) collective-permute-start(bf16[2048,256]{1,0:T(8,128)(2,1)S(1)} %constant_dynamic-update-slice_fusion.rest_0_), channel_id=1, source_target_pairs={{0,1},{1,16},{2,3},{3,18},{4,5},{5,20},{6,7},{7,22},{8,10},{9,11},... | collective-permute-start | bytes 3145736 | tf_op jit(solution)/shard_map/ppermute | solution.py:85
  366.0 3.0 collective-permute-start.11
  424.8 29.2 %collective-permute-start.18 = (bf16[2048,256]{1,0:T(8,128)(2,1)S(1)}, bf16[2048,256]{1,0:T(8,128)(2,1)S(1)}, u32[]{:S(2)}, u32[]{:S(2)}) collective-permute-start(bf16[2048,256]{1,0:T(8,128)(2,1)S(1)} %fusion.3), channel_id=1, source_target_pairs={{0,17},{1,0},{2,19},{3,2},{4,21},{5,4},{6,23},{7,6},{8,14},{9,15},... | collective-permute-start | bytes 3145736 | tf_op jit(solution)/shard_map/ppermute | solution.py:92
  432.2 27.3 %collective-permute-start.19 = (bf16[2048,256]{1,0:T(8,128)(2,1)S(1)}, bf16[2048,256]{1,0:T(8,128)(2,1)S(1)}, u32[]{:S(2)}, u32[]{:S(2)}) collective-permute-start(bf16[2048,256]{1,0:T(8,128)(2,1)S(1)} %fusion.4), channel_id=1, source_target_pairs={{0,1},{1,16},{2,3},{3,18},{4,5},{5,20},{6,7},{7,22},{8,10},{9,11},... | collective-permute-start | bytes 3145736 | tf_op jit(solution)/shard_map/ppermute | solution.py:92
  434.0 25.5 %collective-permute-start.20 = (bf16[2048,256]{1,0:T(8,128)(2,1)S(1)}, bf16[2048,256]{1,0:T(8,128)(2,1)S(1)}, u32[]{:S(2)}, u32[]{:S(2)}) collective-permute-start(bf16[2048,256]{1,0:T(8,128)(2,1)S(1)} %fusion.5), channel_id=1, source_target_pairs={{0,16},{1,17},{2,18},{3,19},{4,20},{5,21},{6,22},{7,23},{8,12},{9,... | collective-permute-start | bytes 3145736 | tf_op jit(solution)/shard_map/ppermute | solution.py:92
  461.7 6.4 %collective-permute-start.21 = (bf16[512,256]{1,0:T(8,128)(2,1)S(1)}, bf16[512,256]{1,0:T(8,128)(2,1)S(1)}, u32[]{:S(2)}, u32[]{:S(2)}) collective-permute-start(bf16[512,256]{1,0:T(8,128)(2,1)S(1)} %get-tuple-element.19), channel_id=1, source_target_pairs={{0,96},{1,97},{2,98},{3,99},{4,100},{5,101},{6,102},{7,103},{8,25}... | collective-permute-start | bytes 786440 | tf_op jit(solution)/shard_map/ppermute | solution.py:92
  462.9 21.8 %collective-permute-start.13 = (bf16[2048,256]{1,0:T(8,128)(2,1)S(1)}, bf16[2048,256]{1,0:T(8,128)(2,1)S(1)}, u32[]{:S(2)}, u32[]{:S(2)}) collective-permute-start(bf16[2048,256]{1,0:T(8,128)(2,1)S(1)} %constant_dynamic-update-slice_fusion.rest_0_), channel_id=1, source_target_pairs={{0,8},{1,9},{2,10},{3,11},{4,12},{5,13},{6,14},{7,15},{8,0},{9,1},... | collective-permute-start | bytes 3145736 | tf_op jit(solution)/shard_map/ppermute | solution.py:62
  463.0 23.9 %collective-permute-start.14 = (bf16[2048,256]{1,0:T(8,128)(2,1)S(1)}, bf16[2048,256]{1,0:T(8,128)(2,1)S(1)}, u32[]{:S(2)}, u32[]{:S(2)}) collective-permute-start(bf16[2048,256]{1,0:T(8,128)(2,1)S(1)} %copy-done.1), channel_id=1, source_target_pairs={{0,8},{1,9},{2,10},{3,11},{4,12},{5,13},{6,14},{7,15},{8,0},{9,1},... | collective-permute-start | bytes 3145736 | tf_op jit(solution)/shard_map/ppermute | solution.py:62
  463.5 25.8 %collective-permute-start.15 = (bf16[2048,256]{1,0:T(8,128)(2,1)S(1)}, bf16[2048,256]{1,0:T(8,128)(2,1)S(1)}, u32[]{:S(2)}, u32[]{:S(2)}) collective-permute-start(bf16[2048,256]{1,0:T(8,128)(2,1)S(1)} %collective-permute-done.7.rest_2_), channel_id=1, source_target_pairs={{0,8},{1,9},{2,10},{3,11},{4,12},{5,13},{6,14},{7,15},{8,0},{9,1},... | collective-permute-start | bytes 3145736 | tf_op jit(solution)/shard_map/ppermute | solution.py:62
  463.5 25.8 %collective-permute-start.16 = (bf16[2048,256]{1,0:T(8,128)(2,1)S(1)}, bf16[2048,256]{1,0:T(8,128)(2,1)S(1)}, u32[]{:S(2)}, u32[]{:S(2)}) collective-permute-start(bf16[2048,256]{1,0:T(8,128)(2,1)S(1)} %collective-permute-done.8.rest_3_), channel_id=1, source_target_pairs={{0,8},{1,9},{2,10},{3,11},{4,12},{5,13},{6,14},{7,15},{8,0},{9,1},... | collective-permute-start | bytes 3145736 | tf_op jit(solution)/shard_map/ppermute | solution.py:62
  468.1 7.6 %collective-permute-start.22 = (bf16[512,256]{1,0:T(8,128)(2,1)S(1)}, bf16[512,256]{1,0:T(8,128)(2,1)S(1)}, u32[]{:S(2)}, u32[]{:S(2)}) collective-permute-start(bf16[512,256]{1,0:T(8,128)(2,1)S(1)} %get-tuple-element.21), channel_id=1, source_target_pairs={{0,32},{1,33},{2,34},{3,35},{4,36},{5,37},{6,38},{7,39},{8,9},{9,2... | collective-permute-start | bytes 786440 | tf_op jit(solution)/shard_map/ppermute | solution.py:92
  475.7 8.8 %collective-permute-start.23 = (bf16[512,256]{1,0:T(8,128)(2,1)S(1)}, bf16[512,256]{1,0:T(8,128)(2,1)S(1)}, u32[]{:S(2)}, u32[]{:S(2)}) collective-permute-start(bf16[512,256]{1,0:T(8,128)(2,1)S(1)} %get-tuple-element.20), channel_id=1, source_target_pairs={{0,64},{1,65},{2,66},{3,67},{4,68},{5,69},{6,70},{7,71},{8,24},{9,... | collective-permute-start | bytes 786440 | tf_op jit(solution)/shard_map/ppermute | solution.py:92
  484.7 14.4 %collective-permute-start.24 = (bf16[128,256]{1,0:T(8,128)(2,1)S(1)}, bf16[128,256]{1,0:T(8,128)(2,1)S(1)}, u32[]{:S(2)}, u32[]{:S(2)}) collective-permute-start(bf16[128,256]{1,0:T(8,128)(2,1)S(1)} %get-tuple-element.22), channel_id=1, source_target_pairs={{0,6},{1,7},{2,0},{3,1},{4,2},{5,3},{6,4},{7,5},{8,104},{9,105},{1... | collective-permute-start | bytes 196616 | tf_op jit(solution)/shard_map/ppermute | solution.py:92
  484.8 14.3 %collective-permute-start.25 = (bf16[128,256]{1,0:T(8,128)(2,1)S(1)}, bf16[128,256]{1,0:T(8,128)(2,1)S(1)}, u32[]{:S(2)}, u32[]{:S(2)}) collective-permute-start(bf16[128,256]{1,0:T(8,128)(2,1)S(1)} %get-tuple-element.24), channel_id=1, source_target_pairs={{0,2},{1,3},{2,4},{3,5},{4,6},{5,7},{6,0},{7,1},{8,40},{9,41},{10,... | collective-permute-start | bytes 196616 | tf_op jit(solution)/shard_map/ppermute | solution.py:92
  486.8 12.3 %collective-permute-start.26 = (bf16[128,256]{1,0:T(8,128)(2,1)S(1)}, bf16[128,256]{1,0:T(8,128)(2,1)S(1)}, u32[]{:S(2)}, u32[]{:S(2)}) collective-permute-start(bf16[128,256]{1,0:T(8,128)(2,1)S(1)} %get-tuple-element.23), channel_id=1, source_target_pairs={{0,4},{1,5},{2,6},{3,7},{4,0},{5,1},{6,2},{7,3},{8,72},{9,73},{10,... | collective-permute-start | bytes 196616 | tf_op jit(solution)/shard_map/ppermute | solution.py:92
  (15 other events, 734.1 us)

commit v2 on v1

--- a/solution.py
+++ b/solution.py
@@ -98,32 +98,35 @@
     return jnp.where(ratio >= 0.5, 1.0, jnp.where(ratio <= -0.5, -1.0, 0.0)).astype(jnp.float32)
 
 
-def shuffle_kernel(table, tokens, own, other, own_sem, other_sem):
+def shuffle_kernel(table, tokens, own, other):
     width = own.shape[1] * 2 // DEVICES
-    for half, (out, sem) in enumerate(((other, other_sem), (own, own_sem))):
-        first = 0 if half else DEVICES // 2
-
-        def start(j, _, out=out, sem=sem, first=first):
+    half = DEVICES // 2
+
+    def move(j, _):
+        target = pl.ds(pl.multiple_of(j * width, width), width)
+        for first, out in ((0, own), (half, other)):
             source = pl.ds(pl.multiple_of(table[first + j] * width, width), width)
-            target = pl.ds(pl.multiple_of(j * width, width), width)
-            pltpu.make_async_copy(tokens.at[:, source], out.at[:, target], sem).start()
-            return 0
-
-        lax.fori_loop(0, DEVICES // 2, start, 0)
-    pltpu.make_async_copy(other, other, other_sem).wait()
-    pltpu.make_async_copy(own, own, own_sem).wait()
+            out[:, target] = tokens[:, source]
+        return 0
+
+    lax.fori_loop(0, half, move, 0, unroll=8)
 
 
 def shuffle(table, tokens):
     rows, features = tokens.shape
+    step_rows = 32
     half = jax.ShapeDtypeStruct((rows, features // 2), tokens.dtype)
-    anywhere = pl.BlockSpec(memory_space=pl.ANY)
+    half_spec = pl.BlockSpec((step_rows, features // 2), lambda i: (i, 0))
     return pl.pallas_call(
         shuffle_kernel,
+        grid=(rows // step_rows,),
         out_shape=(half, half),
-        in_specs=[pl.BlockSpec(memory_space=pltpu.SMEM), anywhere],
-        out_specs=(anywhere, anywhere),
-        scratch_shapes=[pltpu.SemaphoreType.DMA, pltpu.SemaphoreType.DMA],
+        in_specs=[
+            pl.BlockSpec(memory_space=pltpu.SMEM),
+            pl.BlockSpec((step_rows, features), lambda i: (i, 0)),
+        ],
+        out_specs=(half_spec, half_spec),
+        compiler_params=pltpu.CompilerParams(vmem_limit_bytes=16 << 20),
         cost_estimate=pl.CostEstimate(
             flops=0, bytes_accessed=4 * rows * features, transcendentals=0
         ),
@@ -375,13 +378,16 @@
     )
 
     lane = lax.broadcasted_iota(jnp.int32, (1, 128), 1)
-    sums = exchange_sums(
-        jnp.where(
-            lane == 0,
-            jnp.sum(jnp.abs(latent_key)),
-            jnp.where(lane == 1, jnp.sum(jnp.abs(latent_value)), 0.0),
-        )
-    )
+    row = jnp.where(
+        lane == 0,
+        jnp.sum(jnp.abs(latent_key)),
+        jnp.where(lane == 1, jnp.sum(jnp.abs(latent_value)), 0.0),
+    )
+    row, shuffle_table = lax.optimization_barrier((row, table))
+    sums = exchange_sums(row)
+    tokens_own, tokens_other = shuffle(shuffle_table, token_rows)
+    sums, tokens_own, tokens_other = lax.optimization_barrier((sums, tokens_own, tokens_other))
+    tokens_peer = swap_cores(tokens_other)
     entry_count = features * head_size
     key_scale = sums[0, 0] / entry_count + EPSILON
     value_scale = sums[0, 1] / entry_count + EPSILON
@@ -393,8 +399,6 @@
         axis=1,
     )
 
-    tokens_own, tokens_other = shuffle(table, token_rows)
-    tokens_peer = swap_cores(tokens_other)
     for phase in range(2):
         weights = jnp.concatenate(gather_ring(weights, phase), axis=0)
     weight_parts = gather_ring(weights, 2)
@@ -426,6 +430,9 @@
     mixed, query_grad, same_terms, other_terms = attention(
         meta, queries[0], cotangent[0], kv_same, kv_other, head_size, docs, blocks
     )
+    same_terms, other_terms, *other_parts = lax.optimization_barrier(
+        (same_terms, other_terms, *other_parts)
+    )
     chip_terms = (same_terms + swap_cores(other_terms).astype(jnp.float32)).astype(jnp.bfloat16)
     terms = lax.all_to_all(chip_terms, SAME_CORE_CTX, split_axis=0, concat_axis=0, tiled=True)
     grads = jnp.sum(
@@ -437,15 +444,17 @@
         cut = slice(i * part_rows, (i + 1) * part_rows)
         return sum(
             lax.dot_general(
-                rows[:, cut], g, (((0,), (0,)), ((), ())), preferred_element_type=jnp.float32
+                g, rows[:, cut], (((0,), (0,)), ((), ())), preferred_element_type=jnp.float32
             )
             for rows, g in ((tokens_own, grads), (tokens_peer, peer_grads))
         )
 
     summed = reduce_ring([weight_term(i) for i in range(4)], 2)
     token_grad = token_gradient(table, grads, weight_parts + other_parts)
+    summed, token_grad = lax.optimization_barrier((summed, token_grad))
     for phase in (1, 0):
-        summed = reduce_ring(jnp.split(summed, 4, axis=0), phase)
+        summed = reduce_ring(jnp.split(summed, 4, axis=1), phase)
+    summed = summed.T
     return (
         mixed[None],
         query_grad[None],

time: 500 us -> 220 us (0.44)
  Pallas kernels: 280 us -> 38.6 us
  blocking collectives: 77.4 us -> 46.8 us
  waiting for transfers between devices: 83.8 us -> 61 us
  starting transfers between devices: 25.5 us -> 36.1 us
  local copies, waits for them, and re-layouts: 4.85 us -> 13.3 us
  matrix products: 21.9 us -> 15.2 us
    pallas_call x1, Pallas kernels: 256 us -> 4.19 us  [shuffle(): pl.pallas_call(shuffle_kernel, grid=(rows // step_rows,), out_shape=(half...]
    ppermute x9, waiting for transfers between devices: 43 us -> 18.7 us  [reduce_ring(): lax.ppermute(piece.astype(jnp.bfloat16), AXES, along_ring(phase, offset))]
    all_to_all x1 -> x0, blocking collectives: 24.2 us -> none  [exchange_sums(): lax.all_to_all(tile, AXES, split_axis=0, concat_axis=0, tiled=True)]
    all_to_all x0 -> x1, starting transfers between devices: none -> 11.1 us  [exchange_sums(): lax.all_to_all(tile, AXES, split_axis=0, concat_axis=0, tiled=True)]
    pallas_call x1, Pallas kernels: 13.8 us -> 22.7 us  [attention(): pl.pallas_call(functools.partial(attention_kernel, heads=heads, head_size...]
    unnamed x29 -> x35, local copies, waits for them, and re-layouts: 2.19 us -> 11 us
    all_to_all x1, blocking collectives: 29.6 us -> 23.9 us  [body(): lax.all_to_all(chip_terms, SAME_CORE_CTX, split_axis=0, concat_axis=0, ti...]
  transfers between devices with their start and end apart: 27 -> 28, of which waited for: 16 -> 17; matrix products, arithmetic and copies ran while one was open for 3% -> 5% of each run, Pallas kernels for 2% -> 18%
where the time goes in v2:
time: 220 us; the launch traced here: 219 us
  waiting for transfers between devices  61 us (28%)
  blocking collectives  46.8 us (21%)
  Pallas kernels  38.6 us (18%)
  starting transfers between devices  36.1 us (16%)
  matrix products  15.2 us (7%)
  local copies, waits for them, and re-layouts  13.3 us (6%)
  other arithmetic  5.13 us (2%)
  between operations  2.79 us (1%)
    ppermute x9, waiting for transfers between devices, gather_ring(): lax.ppermute(value, AXES, along_ring(phase, -offset))  34.7 us
    all_to_all x1, blocking collectives, body(): lax.all_to_all(chip_terms, SAME_CORE_CTX, split_axis=0, concat_axis=0, ti...  23.9 us
    all_to_all x1, blocking collectives, body(): lax.all_to_all(jnp.broadcast_to(kv_here[None], (groups,) + kv_here.shape)...  22.9 us
    pallas_call x1, Pallas kernels, attention(): pl.pallas_call(functools.partial(attention_kernel, heads=heads, head_size...  22.7 us
    ppermute x9, waiting for transfers between devices, reduce_ring(): lax.ppermute(piece.astype(jnp.bfloat16), AXES, along_ring(phase, offset))  18.7 us
    ppermute x9, starting transfers between devices, reduce_ring(): lax.ppermute(piece.astype(jnp.bfloat16), AXES, along_ring(phase, offset))  13 us
    pallas_call x1, Pallas kernels, token_gradient(): pl.pallas_call(functools.partial(token_grad_kernel, count=len(weights)),...  11.7 us
    all_to_all x1, starting transfers between devices, exchange_sums(): lax.all_to_all(tile, AXES, split_axis=0, concat_axis=0, tiled=True)  11.1 us
  transfers between devices with their start and end apart: 28, of which 17 were waited for; matrix products, arithmetic and copies ran while one was open for 5% of the time, Pallas kernels for 18%

profile of v2, /device:TPU:0, one launch (start us, length us, event | category | flops | bytes accessed | tf_op | source)
XLA Modules:
  0.0 218.9 jit_solution(16322088828036141430)
XLA Ops:
  5.0 11.1 %all-to-all-start = ((f32[128,8,128]{2,1,0:T(8,128)}), f32[128,8,128]{2,1,0:T(8,128)S(1)}, u32[]{:S(2)}, u32[]{:S(2)}) async-start(f32[128,8,128]{2,1,0:T(8,128)} %reshape.64), calls=%async_computation | async-start | bytes 1048576 | tf_op jit(solution)/shard_map/all_to_all | solution.py:359
  16.1 3.4 %copy-done = bf16[1,256,16384]{2,1,0:T(8,128)(2,1)S(1)} copy-done((bf16[1,256,16384]{2,1,0:T(8,128)(2,1)S(1)}, bf16[1,256,16384]{2,1,0:T(8,128)(2,1)}, u32[]{:S(2)}) %copy-start) | copy-done | bytes 8388632
  19.5 4.2 %shuffle_tokens.1 = (bf16[256,8192]{1,0:T(8,128)(2,1)S(1)}, bf16[256,8192]{1,0:T(8,128)(2,1)S(1)}) custom-call(s32[128]{0:T(128)S(1)} %dynamic-slice_bitcast_fusion.table, bf16[256,16384]{1,0:T(8,128)(2,1)S(1)} %bitcast.35), custom_call_target="tpu_custom_call" | custom-call | bytes 16777216 | tf_op jit(solution)/shard_map/shuffle_tokens/pallas_call | solution.py:120
  32.4 2.8 %collective-permute-start.1 = (bf16[128,256]{1,0:T(8,128)(2,1)S(1)}, bf16[128,256]{1,0:T(8,128)(2,1)S(1)}, u32[]{:S(2)}, u32[]{:S(2)}) collective-permute-start(bf16[128,256]{1,0:T(8,128)(2,1)S(1)} %get-tuple-element.63), channel_id=1, source_target_pairs={{0,6},{1,7},{2,0},{3,1},{4,2},{5,3},{6,4},{7,5},{8,104},{9,105},{1... | collective-permute-start | bytes 196616 | tf_op jit(solution)/shard_map/ppermute | solution.py:85
  35.2 2.2 %collective-permute-done = bf16[128,256]{1,0:T(8,128)(2,1)S(1)} collective-permute-done((bf16[128,256]{1,0:T(8,128)(2,1)S(1)}, bf16[128,256]{1,0:T(8,128)(2,1)S(1)}, u32[]{:S(2)}, u32[]{:S(2)}) %collective-permute-start) | collective-permute-done | bytes 65568 | tf_op jit(solution)/shard_map/ppermute | solution.py:85
  37.7 3.3 %collective-permute-done.2 = bf16[128,256]{1,0:T(8,128)(2,1)S(1)} collective-permute-done((bf16[128,256]{1,0:T(8,128)(2,1)S(1)}, bf16[128,256]{1,0:T(8,128)(2,1)S(1)}, u32[]{:S(2)}, u32[]{:S(2)}) %collective-permute-start.2) | collective-permute-done | bytes 65568 | tf_op jit(solution)/shard_map/ppermute | solution.py:85
  41.7 2.6 %collective-permute-start.4 = (bf16[512,256]{1,0:T(8,128)(2,1)S(1)}, bf16[512,256]{1,0:T(8,128)(2,1)S(1)}, u32[]{:S(2)}, u32[]{:S(2)}) collective-permute-start(bf16[512,256]{1,0:T(8,128)(2,1)S(1)} %pad_maximum_fusion), channel_id=1, source_target_pairs={{0,96},{1,97},{2,98},{3,99},{4,100},{5,101},{6,102},{7,103},{8,25}... | collective-permute-start | bytes 786440 | tf_op jit(solution)/shard_map/ppermute | solution.py:85
  44.3 4.3 %collective-permute-done.3 = bf16[512,256]{1,0:T(8,128)(2,1)S(1)} collective-permute-done((bf16[512,256]{1,0:T(8,128)(2,1)S(1)}, bf16[512,256]{1,0:T(8,128)(2,1)S(1)}, u32[]{:S(2)}, u32[]{:S(2)}) %collective-permute-start.3) | collective-permute-done | bytes 262176 | tf_op jit(solution)/shard_map/ppermute | solution.py:85
  48.7 2.4 %collective-permute-done.4 = bf16[512,256]{1,0:T(8,128)(2,1)S(1)} collective-permute-done((bf16[512,256]{1,0:T(8,128)(2,1)S(1)}, bf16[512,256]{1,0:T(8,128)(2,1)S(1)}, u32[]{:S(2)}, u32[]{:S(2)}) %collective-permute-start.4) | collective-permute-done | bytes 262176 | tf_op jit(solution)/shard_map/ppermute | solution.py:85
  56.1 12.6 %collective-permute-done.8.rest_3_ = bf16[2048,256]{1,0:T(8,128)(2,1)S(1)} collective-permute-done((bf16[2048,256]{1,0:T(8,128)(2,1)S(1)}, bf16[2048,256]{1,0:T(8,128)(2,1)S(1)}, u32[]{:S(2)}, u32[]{:S(2)}) %collective-permute-start.8) | collective-permute-done | bytes 1048608 | tf_op jit(solution)/shard_map/ppermute | solution.py:85
  70.3 8.6 %collective-permute-done.7.rest_2_ = bf16[2048,256]{1,0:T(8,128)(2,1)S(1)} collective-permute-done((bf16[2048,256]{1,0:T(8,128)(2,1)S(1)}, bf16[2048,256]{1,0:T(8,128)(2,1)S(1)}, u32[]{:S(2)}, u32[]{:S(2)}) %collective-permute-start.7) | collective-permute-done | bytes 1048608 | tf_op jit(solution)/shard_map/ppermute | solution.py:85
  85.4 22.9 %all_to_all.23 = bf16[8,256,256]{2,1,0:T(8,128)(2,1)} all-to-all(bf16[8,256,256]{2,1,0:T(8,128)(2,1)S(1)} %broadcast_in_dim.69), channel_id=1, replica_groups=mesh['y'=4,'zh'=2,'core'=2,'x'=4,'zl'=2] {'y','zh'}, dimensions={0} | all-to-all | bytes 2097152 | tf_op jit(solution)/shard_map/all_to_all | solution.py:420
  109.5 3.3 %collective-permute-done.11.kv_other = bf16[2048,256]{1,0:T(8,128)(2,1)} collective-permute-done((bf16[2048,256]{1,0:T(8,128)(2,1)}, bf16[2048,256]{1,0:T(8,128)(2,1)}, u32[]{:S(2)}, u32[]{:S(2)}) %collective-permute-start.11) | collective-permute-done | bytes 1048608 | tf_op jit(solution)/shard_map/ppermute | solution.py:62
  114.8 22.7 %masked_attention.1 = (bf16[256,1024]{1,0:T(8,128)(2,1)}, bf16[256,1024]{1,0:T(8,128)(2,1)}, f32[2048,256]{1,0:T(8,128)S(1)}, bf16[2048,256]{1,0:T(8,128)(2,1)S(1)}) custom-call(s32[42]{0:T(128)S(1)} %pad_add_fusion.meta, bf16[256,1024]{1,0:T(8,128)(2,1)S(1)} %bitcast.36, bf16[256,1024]{1,0:T(8,128)(2,1)S(1)} %bitcast.37, ...), custom_call_target="tpu_custom_call" | custom-call | flops 8455716864 | bytes 6291456 | tf_op jit(solution)/shard_map/masked_attention/pallas_call | solution.py:324
  137.7 2.6 %collective-permute-done.16 = bf16[2048,256]{1,0:T(8,128)(2,1)S(1)} collective-permute-done((bf16[2048,256]{1,0:T(8,128)(2,1)S(1)}, bf16[2048,256]{1,0:T(8,128)(2,1)S(1)}, u32[]{:S(2)}, u32[]{:S(2)}) %collective-permute-start.16) | collective-permute-done | bytes 1048608 | tf_op jit(solution)/shard_map/ppermute | solution.py:62
  140.6 23.9 %all_to_all.24 = bf16[8,256,256]{2,1,0:T(8,128)(2,1)} all-to-all(bf16[8,256,256]{2,1,0:T(8,128)(2,1)S(1)} %bitcast.39), channel_id=1, replica_groups=mesh['y'=4,'zh'=2,'core'=2,'x'=4,'zl'=2] {'y','zh'}, dimensions={0} | all-to-all | bytes 2097152 | tf_op jit(solution)/shard_map/all_to_all | solution.py:437
  167.9 2.4 %fusion.27 = f32[256,2048]{1,0:T(8,128)S(1)} fusion(bf16[256,256]{1,0:T(8,128)(2,1)S(1)} %reduce_sum.52.grads, bf16[256,8192]{1,0:T(8,128)(2,1)} %copy-done.1), kind=kOutput, calls=%fused_computation.34 | convolution fusion | flops 268435456 | bytes 3276800 | tf_op jit(solution)/shard_map/dot_general | solution.py:446
  173.6 3.5 %collective-permute-start.18 = (bf16[256,2048]{1,0:T(8,128)(2,1)S(1)}, bf16[256,2048]{1,0:T(8,128)(2,1)S(1)}, u32[]{:S(2)}, u32[]{:S(2)}) collective-permute-start(bf16[256,2048]{1,0:T(8,128)(2,1)S(1)} %fusion.3), channel_id=1, source_target_pairs={{0,17},{1,0},{2,19},{3,2},{4,21},{5,4},{6,23},{7,6},{8,14},{9,15},... | collective-permute-start | bytes 3145736 | tf_op jit(solution)/shard_map/ppermute | solution.py:92
  177.1 11.7 %token_gradient.1 = bf16[256,16384]{1,0:T(8,128)(2,1)} custom-call(s32[128]{0:T(128)S(1)} %dynamic-slice_bitcast_fusion.table, bf16[256,256]{1,0:T(8,128)(2,1)S(1)} %reduce_sum.52.grads, bf16[2048,256]{1,0:T(8,128)(2,1)S(1)} %constant_dynamic-update-slice_fusion.rest_0_, bf16[2048,256]{1,0:T(8,128)(2,1)} %collective-permute-done.6.rest_1_, ...), custom_call_target="tpu_custom_call" | custom-call | flops 2147483648 | bytes 16777216 | tf_op jit(solution)/shard_map/token_gradient/pallas_call | solution.py:170
  189.3 9.6 %collective-permute-done.19 = bf16[256,2048]{1,0:T(8,128)(2,1)S(1)} collective-permute-done((bf16[256,2048]{1,0:T(8,128)(2,1)S(1)}, bf16[256,2048]{1,0:T(8,128)(2,1)S(1)}, u32[]{:S(2)}, u32[]{:S(2)}) %collective-permute-start.19) | collective-permute-done | bytes 1048608 | tf_op jit(solution)/shard_map/ppermute | solution.py:92
  201.9 2.8 %collective-permute-start.21 = (bf16[256,512]{1,0:T(8,128)(2,1)S(1)}, bf16[256,512]{1,0:T(8,128)(2,1)S(1)}, u32[]{:S(2)}, u32[]{:S(2)}) collective-permute-start(bf16[256,512]{1,0:T(8,128)(2,1)S(1)} %get-tuple-element.55), channel_id=1, source_target_pairs={{0,96},{1,97},{2,98},{3,99},{4,100},{5,101},{6,102},{7,103},{8,25}... | collective-permute-start | bytes 786440 | tf_op jit(solution)/shard_map/ppermute | solution.py:92
  204.7 3.3 %collective-permute-done.23 = bf16[256,512]{1,0:T(8,128)(2,1)S(1)} collective-permute-done((bf16[256,512]{1,0:T(8,128)(2,1)S(1)}, bf16[256,512]{1,0:T(8,128)(2,1)S(1)}, u32[]{:S(2)}, u32[]{:S(2)}) %collective-permute-start.23) | collective-permute-done | bytes 262176 | tf_op jit(solution)/shard_map/ppermute | solution.py:92
  208.0 2.7 %collective-permute-done.22 = bf16[256,512]{1,0:T(8,128)(2,1)S(1)} collective-permute-done((bf16[256,512]{1,0:T(8,128)(2,1)S(1)}, bf16[256,512]{1,0:T(8,128)(2,1)S(1)}, u32[]{:S(2)}, u32[]{:S(2)}) %collective-permute-start.22) | collective-permute-done | bytes 262176 | tf_op jit(solution)/shard_map/ppermute | solution.py:92
  214.3 2.6 %collective-permute-done.26 = bf16[256,128]{1,0:T(8,128)(2,1)S(1)} collective-permute-done((bf16[256,128]{1,0:T(8,128)(2,1)S(1)}, bf16[256,128]{1,0:T(8,128)(2,1)S(1)}, u32[]{:S(2)}, u32[]{:S(2)}) %collective-permute-start.26) | collective-permute-done | bytes 65568 | tf_op jit(solution)/shard_map/ppermute | solution.py:92
  (111 shorter events, 44.6 us)
Async XLA Ops:
  5.0 24.3 %all-to-all-start = ((f32[128,8,128]{2,1,0:T(8,128)}), f32[128,8,128]{2,1,0:T(8,128)S(1)}, u32[]{:S(2)}, u32[]{:S(2)}) async-start(f32[128,8,128]{2,1,0:T(8,128)} %reshape.64), calls=%async_computation | async-start | bytes 1048576 | tf_op jit(solution)/shard_map/all_to_all | solution.py:359
  29.5 50.0 %collective-permute-start.9 = (bf16[256,8192]{1,0:T(8,128)(2,1)}, bf16[256,8192]{1,0:T(8,128)(2,1)S(1)}, u32[]{:S(2)}, u32[]{:S(2)}) collective-permute-start(bf16[256,8192]{1,0:T(8,128)(2,1)} %copy-done.4), channel_id=1, source_target_pairs={{0,8},{1,9},{2,10},{3,11},{4,12},{5,13},{6,14},{7,15},{8,0},{9,1},... | collective-permute-start | bytes 12582920 | tf_op jit(solution)/shard_map/ppermute | solution.py:62
  31.9 5.5 %collective-permute-start = (bf16[128,256]{1,0:T(8,128)(2,1)S(1)}, bf16[128,256]{1,0:T(8,128)(2,1)S(1)}, u32[]{:S(2)}, u32[]{:S(2)}) collective-permute-start(bf16[128,256]{1,0:T(8,128)(2,1)S(1)} %get-tuple-element.63), channel_id=1, source_target_pairs={{0,2},{1,3},{2,4},{3,5},{4,6},{5,7},{6,0},{7,1},{8,40},{9,41},{10,... | collective-permute-start | bytes 196616 | tf_op jit(solution)/shard_map/ppermute | solution.py:85
  32.4 5.3 %collective-permute-start.1 = (bf16[128,256]{1,0:T(8,128)(2,1)S(1)}, bf16[128,256]{1,0:T(8,128)(2,1)S(1)}, u32[]{:S(2)}, u32[]{:S(2)}) collective-permute-start(bf16[128,256]{1,0:T(8,128)(2,1)S(1)} %get-tuple-element.63), channel_id=1, source_target_pairs={{0,6},{1,7},{2,0},{3,1},{4,2},{5,3},{6,4},{7,5},{8,104},{9,105},{1... | collective-permute-start | bytes 196616 | tf_op jit(solution)/shard_map/ppermute | solution.py:85
  35.2 5.8 %collective-permute-start.2 = (bf16[128,256]{1,0:T(8,128)(2,1)S(1)}, bf16[128,256]{1,0:T(8,128)(2,1)S(1)}, u32[]{:S(2)}, u32[]{:S(2)}) collective-permute-start(bf16[128,256]{1,0:T(8,128)(2,1)S(1)} %get-tuple-element.63), channel_id=1, source_target_pairs={{0,4},{1,5},{2,6},{3,7},{4,0},{5,1},{6,2},{7,3},{8,72},{9,73},{10,... | collective-permute-start | bytes 196616 | tf_op jit(solution)/shard_map/ppermute | solution.py:85
  41.0 7.7 %collective-permute-start.3 = (bf16[512,256]{1,0:T(8,128)(2,1)S(1)}, bf16[512,256]{1,0:T(8,128)(2,1)S(1)}, u32[]{:S(2)}, u32[]{:S(2)}) collective-permute-start(bf16[512,256]{1,0:T(8,128)(2,1)S(1)} %pad_maximum_fusion), channel_id=1, source_target_pairs={{0,32},{1,33},{2,34},{3,35},{4,36},{5,37},{6,38},{7,39},{8,9},{9,2... | collective-permute-start | bytes 786440 | tf_op jit(solution)/shard_map/ppermute | solution.py:85
  41.7 9.3 %collective-permute-start.4 = (bf16[512,256]{1,0:T(8,128)(2,1)S(1)}, bf16[512,256]{1,0:T(8,128)(2,1)S(1)}, u32[]{:S(2)}, u32[]{:S(2)}) collective-permute-start(bf16[512,256]{1,0:T(8,128)(2,1)S(1)} %pad_maximum_fusion), channel_id=1, source_target_pairs={{0,96},{1,97},{2,98},{3,99},{4,100},{5,101},{6,102},{7,103},{8,25}... | collective-permute-start | bytes 786440 | tf_op jit(solution)/shard_map/ppermute | solution.py:85
  44.3 7.9 %collective-permute-start.5 = (bf16[512,256]{1,0:T(8,128)(2,1)S(1)}, bf16[512,256]{1,0:T(8,128)(2,1)S(1)}, u32[]{:S(2)}, u32[]{:S(2)}) collective-permute-start(bf16[512,256]{1,0:T(8,128)(2,1)S(1)} %pad_maximum_fusion), channel_id=1, source_target_pairs={{0,64},{1,65},{2,66},{3,67},{4,68},{5,69},{6,70},{7,71},{8,24},{9,... | collective-permute-start | bytes 786440 | tf_op jit(solution)/shard_map/ppermute | solution.py:85
  52.2 16.5 %collective-permute-start.8 = (bf16[2048,256]{1,0:T(8,128)(2,1)S(1)}, bf16[2048,256]{1,0:T(8,128)(2,1)S(1)}, u32[]{:S(2)}, u32[]{:S(2)}) collective-permute-start(bf16[2048,256]{1,0:T(8,128)(2,1)S(1)} %constant_dynamic-update-slice_fusion.rest_0_), channel_id=1, source_target_pairs={{0,16},{1,17},{2,18},{3,19},{4,20},{5,21},{6,22},{7,23},{8,12},{9,... | collective-permute-start | bytes 3145736 | tf_op jit(solution)/shard_map/ppermute | solution.py:85
  54.1 24.9 %collective-permute-start.7 = (bf16[2048,256]{1,0:T(8,128)(2,1)S(1)}, bf16[2048,256]{1,0:T(8,128)(2,1)S(1)}, u32[]{:S(2)}, u32[]{:S(2)}) collective-permute-start(bf16[2048,256]{1,0:T(8,128)(2,1)S(1)} %constant_dynamic-update-slice_fusion.rest_0_), channel_id=1, source_target_pairs={{0,17},{1,0},{2,19},{3,2},{4,21},{5,4},{6,23},{7,6},{8,14},{9,15},... | collective-permute-start | bytes 3145736 | tf_op jit(solution)/shard_map/ppermute | solution.py:85
  55.7 24.6 %collective-permute-start.6 = (bf16[2048,256]{1,0:T(8,128)(2,1)S(1)}, bf16[2048,256]{1,0:T(8,128)(2,1)}, u32[]{:S(2)}, u32[]{:S(2)}) collective-permute-start(bf16[2048,256]{1,0:T(8,128)(2,1)S(1)} %constant_dynamic-update-slice_fusion.rest_0_), channel_id=1, source_target_pairs={{0,1},{1,16},{2,3},{3,18},{4,5},{5,20},{6,7},{7,22},{8,10},{9,11},... | collective-permute-start | bytes 3145736 | tf_op jit(solution)/shard_map/ppermute | solution.py:85
  108.3 29.3 %collective-permute-start.12 = (bf16[2048,256]{1,0:T(8,128)(2,1)S(1)}, bf16[2048,256]{1,0:T(8,128)(2,1)}, u32[]{:S(2)}, u32[]{:S(2)}) collective-permute-start(bf16[2048,256]{1,0:T(8,128)(2,1)S(1)} %constant_dynamic-update-slice_fusion.rest_0_), channel_id=1, source_target_pairs={{0,8},{1,9},{2,10},{3,11},{4,12},{5,13},{6,14},{7,15},{8,0},{9,1},... | collective-permute-start | bytes 3145736 | tf_op jit(solution)/shard_map/ppermute | solution.py:62
  108.8 28.8 %collective-permute-start.13 = (bf16[2048,256]{1,0:T(8,128)(2,1)}, bf16[2048,256]{1,0:T(8,128)(2,1)}, u32[]{:S(2)}, u32[]{:S(2)}) collective-permute-start(bf16[2048,256]{1,0:T(8,128)(2,1)} %collective-permute-done.6.rest_1_), channel_id=1, source_target_pairs={{0,8},{1,9},{2,10},{3,11},{4,12},{5,13},{6,14},{7,15},{8,0},{9,1},... | collective-permute-start | bytes 3145736 | tf_op jit(solution)/shard_map/ppermute | solution.py:62
  108.8 28.8 %collective-permute-start.14 = (bf16[2048,256]{1,0:T(8,128)(2,1)S(1)}, bf16[2048,256]{1,0:T(8,128)(2,1)}, u32[]{:S(2)}, u32[]{:S(2)}) collective-permute-start(bf16[2048,256]{1,0:T(8,128)(2,1)S(1)} %collective-permute-done.7.rest_2_), channel_id=1, source_target_pairs={{0,8},{1,9},{2,10},{3,11},{4,12},{5,13},{6,14},{7,15},{8,0},{9,1},... | collective-permute-start | bytes 3145736 | tf_op jit(solution)/shard_map/ppermute | solution.py:62
  109.3 28.3 %collective-permute-start.15 = (bf16[2048,256]{1,0:T(8,128)(2,1)S(1)}, bf16[2048,256]{1,0:T(8,128)(2,1)}, u32[]{:S(2)}, u32[]{:S(2)}) collective-permute-start(bf16[2048,256]{1,0:T(8,128)(2,1)S(1)} %collective-permute-done.8.rest_3_), channel_id=1, source_target_pairs={{0,8},{1,9},{2,10},{3,11},{4,12},{5,13},{6,14},{7,15},{8,0},{9,1},... | collective-permute-start | bytes 3145736 | tf_op jit(solution)/shard_map/ppermute | solution.py:62
  165.9 4.8 %collective-permute-start.17 = (bf16[256,256]{1,0:T(8,128)(2,1)S(1)}, bf16[256,256]{1,0:T(8,128)(2,1)S(1)}, u32[]{:S(2)}, u32[]{:S(2)}) collective-permute-start(bf16[256,256]{1,0:T(8,128)(2,1)S(1)} %reduce_sum.52.grads), channel_id=1, source_target_pairs={{0,8},{1,9},{2,10},{3,11},{4,12},{5,13},{6,14},{7,15},{8,0},{9,1},... | collective-permute-start | bytes 393224 | tf_op jit(solution)/shard_map/ppermute | solution.py:62
  171.3 18.0 %collective-permute-start.20 = (bf16[256,2048]{1,0:T(8,128)(2,1)S(1)}, bf16[256,2048]{1,0:T(8,128)(2,1)S(1)}, u32[]{:S(2)}, u32[]{:S(2)}) collective-permute-start(bf16[256,2048]{1,0:T(8,128)(2,1)S(1)} %fusion.5), channel_id=1, source_target_pairs={{0,16},{1,17},{2,18},{3,19},{4,20},{5,21},{6,22},{7,23},{8,12},{9,... | collective-permute-start | bytes 3145736 | tf_op jit(solution)/shard_map/ppermute | solution.py:92
  173.0 25.9 %collective-permute-start.19 = (bf16[256,2048]{1,0:T(8,128)(2,1)S(1)}, bf16[256,2048]{1,0:T(8,128)(2,1)S(1)}, u32[]{:S(2)}, u32[]{:S(2)}) collective-permute-start(bf16[256,2048]{1,0:T(8,128)(2,1)S(1)} %fusion.4), channel_id=1, source_target_pairs={{0,1},{1,16},{2,3},{3,18},{4,5},{5,20},{6,7},{7,22},{8,10},{9,11},... | collective-permute-start | bytes 3145736 | tf_op jit(solution)/shard_map/ppermute | solution.py:92
  173.6 25.3 %collective-permute-start.18 = (bf16[256,2048]{1,0:T(8,128)(2,1)S(1)}, bf16[256,2048]{1,0:T(8,128)(2,1)S(1)}, u32[]{:S(2)}, u32[]{:S(2)}) collective-permute-start(bf16[256,2048]{1,0:T(8,128)(2,1)S(1)} %fusion.3), channel_id=1, source_target_pairs={{0,17},{1,0},{2,19},{3,2},{4,21},{5,4},{6,23},{7,6},{8,14},{9,15},... | collective-permute-start | bytes 3145736 | tf_op jit(solution)/shard_map/ppermute | solution.py:92
  200.0 8.1 %collective-permute-start.23 = (bf16[256,512]{1,0:T(8,128)(2,1)S(1)}, bf16[256,512]{1,0:T(8,128)(2,1)S(1)}, u32[]{:S(2)}, u32[]{:S(2)}) collective-permute-start(bf16[256,512]{1,0:T(8,128)(2,1)S(1)} %get-tuple-element.56), channel_id=1, source_target_pairs={{0,64},{1,65},{2,66},{3,67},{4,68},{5,69},{6,70},{7,71},{8,24},{9,... | collective-permute-start | bytes 786440 | tf_op jit(solution)/shard_map/ppermute | solution.py:92
  201.5 9.2 %collective-permute-start.22 = (bf16[256,512]{1,0:T(8,128)(2,1)S(1)}, bf16[256,512]{1,0:T(8,128)(2,1)S(1)}, u32[]{:S(2)}, u32[]{:S(2)}) collective-permute-start(bf16[256,512]{1,0:T(8,128)(2,1)S(1)} %get-tuple-element.57), channel_id=1, source_target_pairs={{0,32},{1,33},{2,34},{3,35},{4,36},{5,37},{6,38},{7,39},{8,9},{9,2... | collective-permute-start | bytes 786440 | tf_op jit(solution)/shard_map/ppermute | solution.py:92
  201.9 8.8 %collective-permute-start.21 = (bf16[256,512]{1,0:T(8,128)(2,1)S(1)}, bf16[256,512]{1,0:T(8,128)(2,1)S(1)}, u32[]{:S(2)}, u32[]{:S(2)}) collective-permute-start(bf16[256,512]{1,0:T(8,128)(2,1)S(1)} %get-tuple-element.55), channel_id=1, source_target_pairs={{0,96},{1,97},{2,98},{3,99},{4,100},{5,101},{6,102},{7,103},{8,25}... | collective-permute-start | bytes 786440 | tf_op jit(solution)/shard_map/ppermute | solution.py:92
  210.9 6.0 %collective-permute-start.26 = (bf16[256,128]{1,0:T(8,128)(2,1)S(1)}, bf16[256,128]{1,0:T(8,128)(2,1)S(1)}, u32[]{:S(2)}, u32[]{:S(2)}) collective-permute-start(bf16[256,128]{1,0:T(8,128)(2,1)S(1)} %get-tuple-element.59), channel_id=1, source_target_pairs={{0,4},{1,5},{2,6},{3,7},{4,0},{5,1},{6,2},{7,3},{8,72},{9,73},{10,... | collective-permute-start | bytes 196616 | tf_op jit(solution)/shard_map/ppermute | solution.py:92
  211.0 6.2 %collective-permute-start.25 = (bf16[256,128]{1,0:T(8,128)(2,1)S(1)}, bf16[256,128]{1,0:T(8,128)(2,1)S(1)}, u32[]{:S(2)}, u32[]{:S(2)}) collective-permute-start(bf16[256,128]{1,0:T(8,128)(2,1)S(1)} %get-tuple-element.60), channel_id=1, source_target_pairs={{0,2},{1,3},{2,4},{3,5},{4,6},{5,7},{6,0},{7,1},{8,40},{9,41},{10,... | collective-permute-start | bytes 196616 | tf_op jit(solution)/shard_map/ppermute | solution.py:92
  (18 other events, 188.5 us)

commit v3 on v2

--- a/solution.py
+++ b/solution.py
@@ -19,6 +19,7 @@
 EPSILON = 1e-05
 NEGATIVE = -1e30
 KEY_CHUNK = 256
+STRIP = 32
 
 RING_ORDER = {0: ("x", "y", "z"), 1: ("y", "z", "x")}
 OFFSETS = (0, -1, 1, 2)
@@ -126,7 +127,7 @@
             pl.BlockSpec((step_rows, features), lambda i: (i, 0)),
         ],
         out_specs=(half_spec, half_spec),
-        compiler_params=pltpu.CompilerParams(vmem_limit_bytes=16 << 20),
+        compiler_params=pltpu.CompilerParams(vmem_limit_bytes=56 << 20),
         cost_estimate=pl.CostEstimate(
             flops=0, bytes_accessed=4 * rows * features, transcendentals=0
         ),
@@ -187,13 +188,17 @@
 
 
 def attention_kernel(
-    meta, queries, cotangent, kv_same, kv_other, mixed_out, query_grad, same_out, other_out,
-    keys, values, key_acc, value_acc, scores, q_columns, c_columns, q_rows, c_rows,
+    meta, queries, cotangent, peer_both, kv_same, kv_other,
+    mixed_out, query_grad, same_out, other_out,
+    q_held, c_held, peer_held, kv_held, key_acc, value_acc, scores, prob_grad, low,
+    q_columns, c_columns, q_rows, c_rows, sems,
     *, heads, head_size, block, docs, blocks,
 ):
     scale = head_size ** (-0.5)
     columns = heads * block
     ctx, core = meta[docs + blocks], meta[docs + blocks + 1]
+    own_blocks = q_held.shape[0] // block
+    in_strip = lax.broadcasted_iota(jnp.int32, (STRIP, columns), 0)
     sides = ((kv_same, core, same_out), (kv_other, 1 - core, other_out))
 
     def rows_at(index, size):
@@ -202,23 +207,52 @@
     def true_block(core_of, j):
         return meta[docs + ((j // 2) * 2 + core_of) * 2 + j % 2]
 
-    for ref, core_of, _ in sides:
+    copies = [
+        pltpu.make_async_copy(source, held, sems.at[n])
+        for n, (source, held) in enumerate(
+            ((queries, q_held), (cotangent, c_held), (peer_both, peer_held))
+        )
+    ]
+    for copy in copies:
+        copy.start()
+    for n, (ref, core_of, _) in enumerate(sides):
         for j in range(blocks // 2):
-            target = rows_at(true_block(core_of, j), block)
-            keys[target, :] = ref[j * block : (j + 1) * block, :head_size]
-            values[target, :] = ref[j * block : (j + 1) * block, head_size:]
+            pltpu.make_async_copy(
+                ref.at[j * block : (j + 1) * block, :],
+                kv_held.at[rows_at(true_block(core_of, j), block), :],
+                sems.at[len(copies) + n],
+            ).start()
     key_acc[...] = jnp.zeros_like(key_acc)
     value_acc[...] = jnp.zeros_like(value_acc)
+    for copy in copies:
+        copy.wait()
+    for i in range(2 * own_blocks):
+        here = slice(i % own_blocks * block, (i % own_blocks + 1) * block)
+        for h in range(heads):
+            part = slice(h * block, (h + 1) * block)
+            if i < own_blocks:
+                head = rows_at(core * heads + h, head_size)
+                q, c = q_held[here, head], c_held[here, head]
+            else:
+                q = peer_held[here, h * head_size : (h + 1) * head_size]
+                c = peer_held[here, (heads + h) * head_size : (heads + h + 1) * head_size]
+            q_rows[i, part, :], c_rows[i, part, :] = q, c
+            q_columns[i, :, part], c_columns[i, :, part] = q.T, c.T
+    for n, (ref, _, _) in enumerate(sides):
+        pltpu.make_async_copy(
+            ref, kv_held.at[: blocks // 2 * block, :], sems.at[len(copies) + n]
+        ).wait()
+
+    def keys_at(chunk):
+        return kv_held[rows_at(chunk, KEY_CHUNK), :head_size]
+
+    def values_at(chunk):
+        return kv_held[rows_at(chunk, KEY_CHUNK), head_size:]
 
     def one_block(i, _):
         here = rows_at(i, block)
-        for h in range(heads):
-            head = slice(h * head_size, (h + 1) * head_size)
-            part = slice(h * block, (h + 1) * block)
-            q, c = queries[here, head], cotangent[here, head]
-            q_rows[part, :], c_rows[part, :] = q, c
-            q_columns[:, part], c_columns[:, part] = q.T, c.T
-        start = meta[docs + 2 * ctx + i] * block
+        ctx_of = jnp.where(i < own_blocks, ctx, ctx + 1 - 2 * core)
+        start = meta[docs + own_blocks * ctx_of + lax.rem(i, own_blocks)] * block
         position = start + lax.rem(lax.broadcasted_iota(jnp.int32, (1, columns), 1), block)
         own_start = jnp.zeros((1, columns), jnp.int32)
         first = jnp.int32(0)
@@ -230,17 +264,20 @@
         count = (start + block - 1) // KEY_CHUNK - lowest + 1
 
         def score(c, best):
-            s = scale * jnp.dot(
-                keys[rows_at(lowest + c, KEY_CHUNK), :],
-                q_columns[...],
+            scores[c] = jnp.dot(
+                keys_at(lowest + c),
+                q_columns[i],
                 preferred_element_type=jnp.float32,
             )
-            key_pos = (lowest + c) * KEY_CHUNK + lax.broadcasted_iota(
-                jnp.int32, (KEY_CHUNK, columns), 0
-            )
-            s = jnp.where((key_pos >= own_start) & (key_pos <= position), s, NEGATIVE)
-            scores[c] = s
-            return jnp.maximum(best, jnp.max(s.reshape(KEY_CHUNK // 8, 8, columns), axis=0))
+            first_key = (lowest + c) * KEY_CHUNK
+            for at in range(0, KEY_CHUNK, STRIP):
+                strip = slice(at, at + STRIP)
+                key_pos = first_key + at + in_strip
+                visible = (key_pos >= own_start) & (key_pos <= position)
+                s = jnp.where(visible, scores[c, strip, :] * scale, NEGATIVE)
+                scores[c, strip, :] = s
+                best = jnp.maximum(best, jnp.max(s.reshape(STRIP // 8, 8, columns), axis=0))
+            return best
 
         best = lax.fori_loop(
             0, count, score, jnp.full((8, columns), NEGATIVE, jnp.float32)
@@ -249,12 +286,15 @@
 
         def mix(c, carried):
             total, acc = carried
-            w = jnp.exp(scores[c] - best)
-            scores[c] = w
-            total = total + jnp.sum(w.reshape(KEY_CHUNK // 8, 8, columns), axis=0)
+            for at in range(0, KEY_CHUNK, STRIP):
+                strip = slice(at, at + STRIP)
+                w = jnp.exp(scores[c, strip, :] - best)
+                scores[c, strip, :] = w
+                low[0, strip, :] = w.astype(jnp.bfloat16)
+                total = total + jnp.sum(w.reshape(STRIP // 8, 8, columns), axis=0)
             acc = acc + lax.dot_general(
-                values[rows_at(lowest + c, KEY_CHUNK), :],
-                w.astype(jnp.bfloat16),
+                values_at(lowest + c),
+                low[0],
                 (((0,), (0,)), ((), ())),
                 preferred_element_type=jnp.float32,
             )
@@ -269,7 +309,7 @@
         total = jnp.sum(total, axis=0, keepdims=True)
         mixed = (acc / total).astype(jnp.bfloat16)
         expected = jnp.sum(
-            mixed.astype(jnp.float32) * c_columns[...].astype(jnp.float32), axis=0, keepdims=True
+            mixed.astype(jnp.float32) * c_columns[i].astype(jnp.float32), axis=0, keepdims=True
         )
         per_total = 1.0 / total
         for h in range(heads):
@@ -278,17 +318,22 @@
             ].T
 
         def back(c, q_acc):
-            at = rows_at(lowest + c, KEY_CHUNK)
-            probability = scores[c] * per_total
-            prob_grad = jnp.dot(values[at, :], c_columns[...], preferred_element_type=jnp.float32)
-            score_grad = (probability * (prob_grad - expected)).astype(jnp.bfloat16)
-            key_acc[at, :] += jnp.dot(score_grad, q_rows[...], preferred_element_type=jnp.float32)
-            value_acc[at, :] += jnp.dot(
-                probability.astype(jnp.bfloat16), c_rows[...], preferred_element_type=jnp.float32
-            )
+            chunk = rows_at(lowest + c, KEY_CHUNK)
+            prob_grad[...] = jnp.dot(
+                values_at(lowest + c), c_columns[i], preferred_element_type=jnp.float32
+            )
+            for at in range(0, KEY_CHUNK, STRIP):
+                strip = slice(at, at + STRIP)
+                probability = scores[c, strip, :] * per_total
+                low[0, strip, :] = probability.astype(jnp.bfloat16)
+                low[1, strip, :] = (probability * (prob_grad[strip, :] - expected)).astype(
+                    jnp.bfloat16
+                )
+            value_acc[chunk, :] += jnp.dot(low[0], c_rows[i], preferred_element_type=jnp.float32)
+            key_acc[chunk, :] += jnp.dot(low[1], q_rows[i], preferred_element_type=jnp.float32)
             return q_acc + lax.dot_general(
-                keys[at, :],
-                score_grad,
+                keys_at(lowest + c),
+                low[1],
                 (((0,), (0,)), ((), ())),
                 preferred_element_type=jnp.float32,
             )
@@ -303,7 +348,7 @@
             ].T
         return 0
 
-    lax.fori_loop(0, queries.shape[0] // block, one_block, 0)
+    lax.fori_loop(0, 2 * own_blocks, one_block, 0)
     for _, core_of, out in sides:
         for j in range(blocks // 2):
             source = rows_at(true_block(core_of, j), block)
@@ -312,12 +357,13 @@
             out[part, head_size:] = value_acc[source, :].astype(out.dtype)
 
 
-def attention(meta, queries, cotangent, kv_same, kv_other, head_size, docs, blocks):
+def attention(meta, queries, cotangent, peer_both, kv_same, kv_other, head_size, docs, blocks):
     rows, width = queries.shape
-    heads = width // head_size
+    heads = width // head_size // 2
     length = kv_same.shape[0] + kv_other.shape[0]
     block = length // blocks
     columns = heads * block
+    query_blocks = 2 * rows // block
     in_vmem = pl.BlockSpec(memory_space=pltpu.VMEM)
     most_chunks = 10
     visible = 9 * KEY_CHUNK
@@ -326,38 +372,37 @@
             attention_kernel, heads=heads, head_size=head_size, block=block, docs=docs, blocks=blocks
         ),
         out_shape=(
-            jax.ShapeDtypeStruct((rows, width), jnp.bfloat16),
-            jax.ShapeDtypeStruct((rows, width), jnp.bfloat16),
+            jax.ShapeDtypeStruct((2 * rows, width // 2), jnp.bfloat16),
+            jax.ShapeDtypeStruct((2 * rows, width // 2), jnp.bfloat16),
             jax.ShapeDtypeStruct(kv_same.shape, jnp.float32),
             jax.ShapeDtypeStruct(kv_other.shape, jnp.bfloat16),
         ),
-        in_specs=[pl.BlockSpec(memory_space=pltpu.SMEM)] + [in_vmem] * 4,
+        in_specs=[pl.BlockSpec(memory_space=pltpu.SMEM)] + [pl.BlockSpec(memory_space=pl.ANY)] * 5,
         out_specs=(in_vmem,) * 4,
         scratch_shapes=[
-            pltpu.VMEM((length, head_size), jnp.bfloat16),
-            pltpu.VMEM((length, head_size), jnp.bfloat16),
+            pltpu.VMEM(queries.shape, jnp.bfloat16),
+            pltpu.VMEM(cotangent.shape, jnp.bfloat16),
+            pltpu.VMEM(peer_both.shape, jnp.bfloat16),
+            pltpu.VMEM((length, 2 * head_size), jnp.bfloat16),
             pltpu.VMEM((length, head_size), jnp.float32),
             pltpu.VMEM((length, head_size), jnp.float32),
             pltpu.VMEM((most_chunks, KEY_CHUNK, columns), jnp.float32),
-            pltpu.VMEM((head_size, columns), jnp.bfloat16),
-            pltpu.VMEM((head_size, columns), jnp.bfloat16),
-            pltpu.VMEM((columns, head_size), jnp.bfloat16),
-            pltpu.VMEM((columns, head_size), jnp.bfloat16),
+            pltpu.VMEM((KEY_CHUNK, columns), jnp.float32),
+            pltpu.VMEM((2, KEY_CHUNK, columns), jnp.bfloat16),
+            pltpu.VMEM((query_blocks, head_size, columns), jnp.bfloat16),
+            pltpu.VMEM((query_blocks, head_size, columns), jnp.bfloat16),
+            pltpu.VMEM((query_blocks, columns, head_size), jnp.bfloat16),
+            pltpu.VMEM((query_blocks, columns, head_size), jnp.bfloat16),
+            pltpu.SemaphoreType.DMA((5,)),
         ],
         compiler_params=pltpu.CompilerParams(vmem_limit_bytes=40 << 20),
         cost_estimate=pl.CostEstimate(
-            flops=14 * rows * heads * visible * head_size,
+            flops=28 * rows * heads * visible * head_size,
             bytes_accessed=8 * rows * width + 8 * length * head_size,
-            transcendentals=rows * heads * visible,
+            transcendentals=2 * rows * heads * visible,
         ),
         name="masked_attention",
-    )(meta, queries, cotangent, kv_same, kv_other)
-
-
-def exchange_sums(row):
-    tile = jnp.broadcast_to(row[None], (DEVICES, 8, row.shape[1])).reshape(-1, row.shape[1])
-    everyones = lax.all_to_all(tile, AXES, split_axis=0, concat_axis=0, tiled=True)
-    return jnp.sum(everyones.reshape(DEVICES, 8, row.shape[1]), axis=0)[:1]
+    )(meta, queries, cotangent, peer_both, kv_same, kv_other)
 
 
 def body(tokens, queries, cotangent, latent_key, latent_value, lengths, block_order):
@@ -377,30 +422,40 @@
         ]
     )
 
-    lane = lax.broadcasted_iota(jnp.int32, (1, 128), 1)
-    row = jnp.where(
-        lane == 0,
-        jnp.sum(jnp.abs(latent_key)),
-        jnp.where(lane == 1, jnp.sum(jnp.abs(latent_value)), 0.0),
-    )
-    row, shuffle_table = lax.optimization_barrier((row, table))
-    sums = exchange_sums(row)
-    tokens_own, tokens_other = shuffle(shuffle_table, token_rows)
-    sums, tokens_own, tokens_other = lax.optimization_barrier((sums, tokens_own, tokens_other))
+    core = lax.axis_index("core")
+    peer_both = swap_cores(
+        jnp.concatenate(
+            [
+                lax.dynamic_slice_in_dim(a[0], (1 - core) * a.shape[2] // 2, a.shape[2] // 2, 1)
+                for a in (queries, cotangent)
+            ],
+            axis=1,
+        )
+    )
+    latents = jnp.concatenate([latent_key, latent_value], axis=1)
+    for phase in range(2):
+        latents = jnp.concatenate(gather_ring(latents, phase), axis=0)
+    tokens_own, tokens_other = shuffle(table, token_rows)
+    latents, tokens_own, tokens_other, peer_both, meta = lax.optimization_barrier(
+        (latents, tokens_own, tokens_other, peer_both, meta)
+    )
     tokens_peer = swap_cores(tokens_other)
+    sums = jnp.broadcast_to(jnp.sum(jnp.abs(latents), axis=0, keepdims=True), (8, 2 * head_size))
+    sums = sum(gather_ring(sums, 2))
+    sums = sums + swap_cores(sums)
     entry_count = features * head_size
-    key_scale = sums[0, 0] / entry_count + EPSILON
-    value_scale = sums[0, 1] / entry_count + EPSILON
+    key_scale = jnp.sum(sums[0, :head_size]) / entry_count + EPSILON
+    value_scale = jnp.sum(sums[0, head_size:]) / entry_count + EPSILON
     weights = jnp.concatenate(
         [
-            (key_scale * levels(latent_key / key_scale)).astype(jnp.bfloat16),
-            (value_scale * levels(latent_value / value_scale)).astype(jnp.bfloat16),
+            (scale * levels(latent / scale)).astype(jnp.bfloat16)
+            for latent, scale in (
+                (latents[:, :head_size], key_scale),
+                (latents[:, head_size:], value_scale),
+            )
         ],
         axis=1,
     )
-
-    for phase in range(2):
-        weights = jnp.concatenate(gather_ring(weights, phase), axis=0)
     weight_parts = gather_ring(weights, 2)
     part_rows = weights.shape[0]
 
@@ -428,7 +483,7 @@
     other_parts = [swap_cores(part) for part in weight_parts]
 
     mixed, query_grad, same_terms, other_terms = attention(
-        meta, queries[0], cotangent[0], kv_same, kv_other, head_size, docs, blocks
+        meta, queries[0], cotangent[0], peer_both, kv_same, kv_other, head_size, docs, blocks
     )
     same_terms, other_terms, *other_parts = lax.optimization_barrier(
         (same_terms, other_terms, *other_parts)
@@ -452,6 +507,16 @@
     summed = reduce_ring([weight_term(i) for i in range(4)], 2)
     token_grad = token_gradient(table, grads, weight_parts + other_parts)
     summed, token_grad = lax.optimization_barrier((summed, token_grad))
+    from_peer = swap_cores(jnp.concatenate([mixed[rows_here:], query_grad[rows_here:]], axis=1))
+
+    def both_halves(own, peers):
+        return jnp.concatenate(
+            [jnp.where(core == 0, own, peers), jnp.where(core == 0, peers, own)], axis=1
+        )
+
+    half_width = mixed.shape[1]
+    mixed = both_halves(mixed[:rows_here], from_peer[:, :half_width])
+    query_grad = both_halves(query_grad[:rows_here], from_peer[:, half_width:])
     for phase in (1, 0):
         summed = reduce_ring(jnp.split(summed, 4, axis=1), phase)
     summed = summed.T

time: 220 us -> 229 us (1.041); the launches traced: 219 us -> 225 us
  matrix products: 15.2 us -> 23.9 us
  waiting for transfers between devices: 61 us -> 52.6 us
  starting transfers between devices: 36.1 us -> 41.9 us
    ppermute x9, waiting for transfers between devices: 18.7 us -> 6.94 us  [reduce_ring(): lax.ppermute(piece.astype(jnp.bfloat16), AXES, along_ring(phase, offset))]
    all_to_all x1 -> x0, starting transfers between devices: 11.1 us -> none  [exchange_sums(): lax.all_to_all(tile, AXES, split_axis=0, concat_axis=0, tiled=True)]
    ppermute x9 -> x12, starting transfers between devices: 10.5 us -> 21 us  [gather_ring(): lax.ppermute(value, AXES, along_ring(phase, -offset))]
    dot_general x8, matrix products: 7.43 us -> 15.5 us  [weight_term(): lax.dot_general(g, rows[:, cut], (((0,), (0,)), ((), ())), preferred_elem...]
    pallas_call x1, Pallas kernels: 4.19 us -> 10.4 us  [shuffle(): pl.pallas_call(shuffle_kernel, grid=(rows // step_rows,), out_shape=(half...]
    pallas_call x1, Pallas kernels: 22.7 us -> 16.8 us  [attention(): pl.pallas_call(functools.partial(attention_kernel, heads=heads, head_size...]
    ppermute x9, starting transfers between devices: 13 us -> 19 us  [reduce_ring(): lax.ppermute(piece.astype(jnp.bfloat16), AXES, along_ring(phase, offset))]
    ppermute x9 -> x12, waiting for transfers between devices: 34.7 us -> 37.9 us  [gather_ring(): lax.ppermute(value, AXES, along_ring(phase, -offset))]
  transfers between devices with their start and end apart: 28 -> 33, of which waited for: 17 -> 14; matrix products, arithmetic and copies ran while one was open for 5% -> 11% of each run, Pallas kernels for 18% -> 16%
where the time goes in v3:
time: 229 us; the launch traced here: 225 us
  waiting for transfers between devices  52.6 us (23%)
  blocking collectives  45.8 us (20%)
  starting transfers between devices  41.9 us (18%)
  Pallas kernels  36.9 us (16%)
  matrix products  23.9 us (10%)
  local copies, waits for them, and re-layouts  14.8 us (6%)
  other arithmetic  6.44 us (3%)
  between operations  2.58 us (1%)
    ppermute x12, waiting for transfers between devices, gather_ring(): lax.ppermute(value, AXES, along_ring(phase, -offset))  37.9 us
    all_to_all x1, blocking collectives, body(): lax.all_to_all(chip_terms, SAME_CORE_CTX, split_axis=0, concat_axis=0, ti...  24.9 us
    ppermute x12, starting transfers between devices, gather_ring(): lax.ppermute(value, AXES, along_ring(phase, -offset))  21 us
    all_to_all x1, blocking collectives, body(): lax.all_to_all(jnp.broadcast_to(kv_here[None], (groups,) + kv_here.shape)...  20.9 us
    ppermute x9, starting transfers between devices, reduce_ring(): lax.ppermute(piece.astype(jnp.bfloat16), AXES, along_ring(phase, offset))  19 us
    pallas_call x1, Pallas kernels, attention(): pl.pallas_call(functools.partial(attention_kernel, heads=heads, head_size...  16.8 us
    dot_general x8, matrix products, weight_term(): lax.dot_general(g, rows[:, cut], (((0,), (0,)), ((), ())), preferred_elem...  15.5 us
    pallas_call x1, Pallas kernels, shuffle(): pl.pallas_call(shuffle_kernel, grid=(rows // step_rows,), out_shape=(half...  10.4 us
  transfers between devices with their start and end apart: 33, of which 14 were waited for; matrix products, arithmetic and copies ran while one was open for 11% of the time, Pallas kernels for 16%

profile of v3, /device:TPU:0, one launch (start us, length us, event | category | flops | bytes accessed | tf_op | source)
XLA Modules:
  0.0 224.9 jit_solution(13805268265598903907)
XLA Ops:
  6.9 1.9 collective-permute-start.2
  10.4 3.2 %collective-permute-done.2 = f32[128,256]{1,0:T(8,128)S(1)} collective-permute-done((f32[128,256]{1,0:T(8,128)}, f32[128,256]{1,0:T(8,128)S(1)}, u32[]{:S(2)}, u32[]{:S(2)}) %collective-permute-start.2) | collective-permute-done | bytes 131104 | tf_op jit(solution)/shard_map/ppermute | solution.py:86
  14.5 1.7 collective-permute-start.3
  19.2 10.4 %shuffle_tokens.1 = (bf16[256,8192]{1,0:T(8,128)(2,1)}, bf16[256,8192]{1,0:T(8,128)(2,1)}) custom-call(s32[128]{0:T(128)} %fusion.39.table, bf16[256,16384]{1,0:T(8,128)(2,1)} %bitcast.41), custom_call_target="tpu_custom_call" | custom-call | bytes 16777216 | tf_op jit(solution)/shard_map/shuffle_tokens/pallas_call | solution.py:121
  29.6 2.1 collective-permute-start.5
  31.8 8.5 %collective-permute-done.5 = f32[512,256]{1,0:T(8,128)S(1)} collective-permute-done((f32[512,256]{1,0:T(8,128)S(1)}, f32[512,256]{1,0:T(8,128)S(1)}, u32[]{:S(2)}, u32[]{:S(2)}) %collective-permute-start.5) | collective-permute-done | bytes 524320 | tf_op jit(solution)/shard_map/ppermute | solution.py:86
  40.7 4.0 %collective-permute-start.9 = (f32[8,256]{1,0:T(8,128)S(1)}, f32[8,256]{1,0:T(8,128)S(1)}, u32[]{:S(2)}, u32[]{:S(2)}) collective-permute-start(f32[8,256]{1,0:T(8,128)S(1)} %broadcast_in_dim.53), channel_id=1, source_target_pairs={{0,16},{1,17},{2,18},{3,19},{4,20},{5,21},{6,22},{7,23},{8,12},{9,... | collective-permute-start | bytes 24584 | tf_op jit(solution)/shard_map/ppermute | solution.py:86
  48.4 1.9 collective-permute-done.7
  55.9 2.7 %collective-permute-start.12 = (bf16[2048,256]{1,0:T(8,128)(2,1)S(1)}, bf16[2048,256]{1,0:T(8,128)(2,1)S(1)}, u32[]{:S(2)}, u32[]{:S(2)}) collective-permute-start(bf16[2048,256]{1,0:T(8,128)(2,1)S(1)} %pad_maximum_fusion.rest_0_), channel_id=1, source_target_pairs={{0,17},{1,0},{2,19},{3,2},{4,21},{5,4},{6,23},{7,6},{8,14},{9,15},... | collective-permute-start | bytes 3145736 | tf_op jit(solution)/shard_map/ppermute | solution.py:86
  58.6 12.0 %collective-permute-done.13.rest_3_ = bf16[2048,256]{1,0:T(8,128)(2,1)S(1)} collective-permute-done((bf16[2048,256]{1,0:T(8,128)(2,1)S(1)}, bf16[2048,256]{1,0:T(8,128)(2,1)S(1)}, u32[]{:S(2)}, u32[]{:S(2)}) %collective-permute-start.13) | collective-permute-done | bytes 1048608 | tf_op jit(solution)/shard_map/ppermute | solution.py:86
  71.0 10.7 %collective-permute-done.11.rest_1_ = bf16[2048,256]{1,0:T(8,128)(2,1)S(1)} collective-permute-done((bf16[2048,256]{1,0:T(8,128)(2,1)S(1)}, bf16[2048,256]{1,0:T(8,128)(2,1)S(1)}, u32[]{:S(2)}, u32[]{:S(2)}) %collective-permute-start.11) | collective-permute-done | bytes 1048608 | tf_op jit(solution)/shard_map/ppermute | solution.py:86
  91.0 20.9 %all_to_all.17 = bf16[8,256,256]{2,1,0:T(8,128)(2,1)S(1)} all-to-all(bf16[8,256,256]{2,1,0:T(8,128)(2,1)S(1)} %broadcast_in_dim.57), channel_id=1, replica_groups=mesh['y'=4,'zh'=2,'core'=2,'x'=4,'zl'=2] {'y','zh'}, dimensions={0} | all-to-all | bytes 2097152 | tf_op jit(solution)/shard_map/all_to_all | solution.py:475
  114.6 16.8 %masked_attention.1 = (bf16[512,512]{1,0:T(8,128)(2,1)S(1)}, bf16[512,512]{1,0:T(8,128)(2,1)S(1)}, f32[2048,256]{1,0:T(8,128)S(1)}, bf16[2048,256]{1,0:T(8,128)(2,1)S(1)}) custom-call(s32[42]{0:T(128)S(1)} %pad_add_fusion.meta, bf16[256,1024]{1,0:T(8,128)(2,1)S(1)} %bitcast.38, bf16[256,1024]{1,0:T(8,128)(2,1)S(1)} %bitcast.39, ...), custom_call_target="tpu_custom_call" | custom-call | flops 8455716864 | bytes 6291456 | tf_op jit(solution)/shard_map/masked_attention/pallas_call | solution.py:370
  133.3 2.5 %collective-permute-done.22 = bf16[2048,256]{1,0:T(8,128)(2,1)S(1)} collective-permute-done((bf16[2048,256]{1,0:T(8,128)(2,1)S(1)}, bf16[2048,256]{1,0:T(8,128)(2,1)S(1)}, u32[]{:S(2)}, u32[]{:S(2)}) %collective-permute-start.22) | collective-permute-done | bytes 1048608 | tf_op jit(solution)/shard_map/ppermute | solution.py:63
  136.1 24.9 %all_to_all.18 = bf16[8,256,256]{2,1,0:T(8,128)(2,1)} all-to-all(bf16[8,256,256]{2,1,0:T(8,128)(2,1)S(1)} %bitcast.42), channel_id=1, replica_groups=mesh['y'=4,'zh'=2,'core'=2,'x'=4,'zl'=2] {'y','zh'}, dimensions={0} | all-to-all | bytes 2097152 | tf_op jit(solution)/shard_map/all_to_all | solution.py:492
  165.4 2.8 %fusion.5 = bf16[256,2048]{1,0:T(8,128)(2,1)} fusion(f32[256,2048]{1,0:T(8,128)S(1)} %fusion.11, bf16[256,256]{1,0:T(8,128)(2,1)S(1)} %reduce_sum.52.grads, bf16[256,8192]{1,0:T(8,128)(2,1)} %get-tuple-element.28), kind=kOutput, calls=%fused_computation.9 | convolution fusion | flops 269484032 | bytes 4325376 | tf_op jit(solution)/shard_map/dot_general | solution.py:501
  177.0 2.0 collective-permute-start.24
  185.2 9.7 %token_gradient.1 = bf16[256,16384]{1,0:T(8,128)(2,1)} custom-call(s32[128]{0:T(128)S(1)} %copy-done.16, bf16[256,256]{1,0:T(8,128)(2,1)S(1)} %reduce_sum.52.grads, bf16[2048,256]{1,0:T(8,128)(2,1)S(1)} %pad_maximum_fusion.rest_0_, bf16[2048,256]{1,0:T(8,128)(2,1)S(1)} %copy-done.1, bf16[2048,256]{1,0:T(8,128)(2,1)S(1)} %collective-permute-done.12.rest_2_, ...), custom_call_target="tpu_custom_call" | custom-call | flops 2147483648 | bytes 16777216 | tf_op jit(solution)/shard_map/token_gradient/pallas_call | solution.py:171
  196.6 3.0 %fusion.2 = f32[256,2048]{1,0:T(8,128)S(1)} fusion(f32[256,2048]{1,0:T(8,128)S(1)} %fusion.23, bf16[256,256]{1,0:T(8,128)(2,1)S(1)} %reduce_sum.52.grads, bf16[256,2048]{1,0:T(8,128)(2,1)} %collective-permute-done.26, bf16[256,2048]{1,0:T(8,128)(2,1)} %collective-permute-done.25, bf16[256,2048]{1,0:T(8,128)(2,1)} %collective-permute-done.24, ...), kind=kOutput, calls=%fused_computation.6 | convolution fusion | flops 272105472 | bytes 8519680 | tf_op jit(solution)/shard_map/dot_general | solution.py:501
  202.0 2.2 collective-permute-start.27
  205.2 2.8 %collective-permute-done.29 = bf16[256,512]{1,0:T(8,128)(2,1)S(1)} collective-permute-done((bf16[256,512]{1,0:T(8,128)(2,1)S(1)}, bf16[256,512]{1,0:T(8,128)(2,1)S(1)}, u32[]{:S(2)}, u32[]{:S(2)}) %collective-permute-start.29) | collective-permute-done | bytes 262176 | tf_op jit(solution)/shard_map/ppermute | solution.py:93
  208.0 2.7 %collective-permute-done.28 = bf16[256,512]{1,0:T(8,128)(2,1)S(1)} collective-permute-done((bf16[256,512]{1,0:T(8,128)(2,1)S(1)}, bf16[256,512]{1,0:T(8,128)(2,1)S(1)}, u32[]{:S(2)}, u32[]{:S(2)}) %collective-permute-start.28) | collective-permute-done | bytes 262176 | tf_op jit(solution)/shard_map/ppermute | solution.py:93
  210.9 7.0 %collective-permute-start.32 = (bf16[256,128]{1,0:T(8,128)(2,1)S(1)}, bf16[256,128]{1,0:T(8,128)(2,1)S(1)}, u32[]{:S(2)}, u32[]{:S(2)}) collective-permute-start(bf16[256,128]{1,0:T(8,128)(2,1)S(1)} %get-tuple-element.69), channel_id=1, source_target_pairs={{0,4},{1,5},{2,6},{3,7},{4,0},{5,1},{6,2},{7,3},{8,72},{9,73},{10,... | collective-permute-start | bytes 196616 | tf_op jit(solution)/shard_map/ppermute | solution.py:93
  217.9 3.2 %collective-permute-start.30 = (bf16[256,128]{1,0:T(8,128)(2,1)S(1)}, bf16[256,128]{1,0:T(8,128)(2,1)S(1)}, u32[]{:S(2)}, u32[]{:S(2)}) collective-permute-start(bf16[256,128]{1,0:T(8,128)(2,1)S(1)} %get-tuple-element.68), channel_id=1, source_target_pairs={{0,6},{1,7},{2,0},{3,1},{4,2},{5,3},{6,4},{7,5},{8,104},{9,105},{1... | collective-permute-start | bytes 196616 | tf_op jit(solution)/shard_map/ppermute | solution.py:93
  (149 shorter events, 62.5 us)
Async XLA Ops:
  3.6 6.7 %collective-permute-start = (f32[128,256]{1,0:T(8,128)}, f32[128,256]{1,0:T(8,128)S(1)}, u32[]{:S(2)}, u32[]{:S(2)}) collective-permute-start(f32[128,256]{1,0:T(8,128)} %get-tuple-element.73), channel_id=1, source_target_pairs={{0,2},{1,3},{2,4},{3,5},{4,6},{5,7},{6,0},{7,1},{8,40},{9,41},{10,... | collective-permute-start | bytes 393224 | tf_op jit(solution)/shard_map/ppermute | solution.py:86
  6.9 6.7 %collective-permute-start.2 = (f32[128,256]{1,0:T(8,128)}, f32[128,256]{1,0:T(8,128)S(1)}, u32[]{:S(2)}, u32[]{:S(2)}) collective-permute-start(f32[128,256]{1,0:T(8,128)} %get-tuple-element.73), channel_id=1, source_target_pairs={{0,4},{1,5},{2,6},{3,7},{4,0},{5,1},{6,2},{7,3},{8,72},{9,73},{10,... | collective-permute-start | bytes 393224 | tf_op jit(solution)/shard_map/ppermute | solution.py:86
  10.1 30.2 %collective-permute-start.6 = (bf16[256,1024]{1,0:T(8,128)(2,1)S(1)}, bf16[256,1024]{1,0:T(8,128)(2,1)S(1)}, u32[]{:S(2)}, u32[]{:S(2)}) collective-permute-start(bf16[256,1024]{1,0:T(8,128)(2,1)S(1)} %pad_maximum_fusion.2), channel_id=1, source_target_pairs={{0,8},{1,9},{2,10},{3,11},{4,12},{5,13},{6,14},{7,15},{8,0},{9,1},... | collective-permute-start | bytes 1572872 | tf_op jit(solution)/shard_map/ppermute | solution.py:63
  14.5 17.2 %collective-permute-start.3 = (f32[512,256]{1,0:T(8,128)S(1)}, f32[512,256]{1,0:T(8,128)S(1)}, u32[]{:S(2)}, u32[]{:S(2)}) collective-permute-start(f32[512,256]{1,0:T(8,128)S(1)} %pad_maximum_fusion.1), channel_id=1, source_target_pairs={{0,32},{1,33},{2,34},{3,35},{4,36},{5,37},{6,38},{7,39},{8,9},{9,2... | collective-permute-start | bytes 1572872 | tf_op jit(solution)/shard_map/ppermute | solution.py:86
  17.5 14.3 %collective-permute-start.4 = (f32[512,256]{1,0:T(8,128)S(1)}, f32[512,256]{1,0:T(8,128)S(1)}, u32[]{:S(2)}, u32[]{:S(2)}) collective-permute-start(f32[512,256]{1,0:T(8,128)S(1)} %pad_maximum_fusion.1), channel_id=1, source_target_pairs={{0,96},{1,97},{2,98},{3,99},{4,100},{5,101},{6,102},{7,103},{8,25}... | collective-permute-start | bytes 1572872 | tf_op jit(solution)/shard_map/ppermute | solution.py:86
  29.6 10.7 %collective-permute-start.5 = (f32[512,256]{1,0:T(8,128)S(1)}, f32[512,256]{1,0:T(8,128)S(1)}, u32[]{:S(2)}, u32[]{:S(2)}) collective-permute-start(f32[512,256]{1,0:T(8,128)S(1)} %pad_maximum_fusion.1), channel_id=1, source_target_pairs={{0,64},{1,65},{2,66},{3,67},{4,68},{5,69},{6,70},{7,71},{8,24},{9,... | collective-permute-start | bytes 1572872 | tf_op jit(solution)/shard_map/ppermute | solution.py:86
  40.3 41.8 %collective-permute-start.14 = (bf16[256,8192]{1,0:T(8,128)(2,1)}, bf16[256,8192]{1,0:T(8,128)(2,1)}, u32[]{:S(2)}, u32[]{:S(2)}) collective-permute-start(bf16[256,8192]{1,0:T(8,128)(2,1)} %get-tuple-element.30), channel_id=1, source_target_pairs={{0,8},{1,9},{2,10},{3,11},{4,12},{5,13},{6,14},{7,15},{8,0},{9,1},... | collective-permute-start | bytes 12582920 | tf_op jit(solution)/shard_map/ppermute | solution.py:63
  40.7 6.1 %collective-permute-start.9 = (f32[8,256]{1,0:T(8,128)S(1)}, f32[8,256]{1,0:T(8,128)S(1)}, u32[]{:S(2)}, u32[]{:S(2)}) collective-permute-start(f32[8,256]{1,0:T(8,128)S(1)} %broadcast_in_dim.53), channel_id=1, source_target_pairs={{0,16},{1,17},{2,18},{3,19},{4,20},{5,21},{6,22},{7,23},{8,12},{9,... | collective-permute-start | bytes 24584 | tf_op jit(solution)/shard_map/ppermute | solution.py:86
  54.1 16.5 %collective-permute-start.13 = (bf16[2048,256]{1,0:T(8,128)(2,1)S(1)}, bf16[2048,256]{1,0:T(8,128)(2,1)S(1)}, u32[]{:S(2)}, u32[]{:S(2)}) collective-permute-start(bf16[2048,256]{1,0:T(8,128)(2,1)S(1)} %pad_maximum_fusion.rest_0_), channel_id=1, source_target_pairs={{0,16},{1,17},{2,18},{3,19},{4,20},{5,21},{6,22},{7,23},{8,12},{9,... | collective-permute-start | bytes 3145736 | tf_op jit(solution)/shard_map/ppermute | solution.py:86
  55.3 26.4 %collective-permute-start.11 = (bf16[2048,256]{1,0:T(8,128)(2,1)S(1)}, bf16[2048,256]{1,0:T(8,128)(2,1)S(1)}, u32[]{:S(2)}, u32[]{:S(2)}) collective-permute-start(bf16[2048,256]{1,0:T(8,128)(2,1)S(1)} %pad_maximum_fusion.rest_0_), channel_id=1, source_target_pairs={{0,1},{1,16},{2,3},{3,18},{4,5},{5,20},{6,7},{7,22},{8,10},{9,11},... | collective-permute-start | bytes 3145736 | tf_op jit(solution)/shard_map/ppermute | solution.py:86
  55.9 29.6 %collective-permute-start.12 = (bf16[2048,256]{1,0:T(8,128)(2,1)S(1)}, bf16[2048,256]{1,0:T(8,128)(2,1)S(1)}, u32[]{:S(2)}, u32[]{:S(2)}) collective-permute-start(bf16[2048,256]{1,0:T(8,128)(2,1)S(1)} %pad_maximum_fusion.rest_0_), channel_id=1, source_target_pairs={{0,17},{1,0},{2,19},{3,2},{4,21},{5,4},{6,23},{7,6},{8,14},{9,15},... | collective-permute-start | bytes 3145736 | tf_op jit(solution)/shard_map/ppermute | solution.py:86
  111.9 21.0 %collective-permute-start.18 = (bf16[2048,256]{1,0:T(8,128)(2,1)S(1)}, bf16[2048,256]{1,0:T(8,128)(2,1)S(1)}, u32[]{:S(2)}, u32[]{:S(2)}) collective-permute-start(bf16[2048,256]{1,0:T(8,128)(2,1)S(1)} %pad_maximum_fusion.rest_0_), channel_id=1, source_target_pairs={{0,8},{1,9},{2,10},{3,11},{4,12},{5,13},{6,14},{7,15},{8,0},{9,1},... | collective-permute-start | bytes 3145736 | tf_op jit(solution)/shard_map/ppermute | solution.py:63
  112.5 20.5 %collective-permute-start.19 = (bf16[2048,256]{1,0:T(8,128)(2,1)S(1)}, bf16[2048,256]{1,0:T(8,128)(2,1)S(1)}, u32[]{:S(2)}, u32[]{:S(2)}) collective-permute-start(bf16[2048,256]{1,0:T(8,128)(2,1)S(1)} %collective-permute-done.11.rest_1_), channel_id=1, source_target_pairs={{0,8},{1,9},{2,10},{3,11},{4,12},{5,13},{6,14},{7,15},{8,0},{9,1},... | collective-permute-start | bytes 3145736 | tf_op jit(solution)/shard_map/ppermute | solution.py:63
  112.5 20.6 %collective-permute-start.20 = (bf16[2048,256]{1,0:T(8,128)(2,1)S(1)}, bf16[2048,256]{1,0:T(8,128)(2,1)S(1)}, u32[]{:S(2)}, u32[]{:S(2)}) collective-permute-start(bf16[2048,256]{1,0:T(8,128)(2,1)S(1)} %collective-permute-done.12.rest_2_), channel_id=1, source_target_pairs={{0,8},{1,9},{2,10},{3,11},{4,12},{5,13},{6,14},{7,15},{8,0},{9,1},... | collective-permute-start | bytes 3145736 | tf_op jit(solution)/shard_map/ppermute | solution.py:63
  113.0 20.1 %collective-permute-start.21 = (bf16[2048,256]{1,0:T(8,128)(2,1)S(1)}, bf16[2048,256]{1,0:T(8,128)(2,1)S(1)}, u32[]{:S(2)}, u32[]{:S(2)}) collective-permute-start(bf16[2048,256]{1,0:T(8,128)(2,1)S(1)} %collective-permute-done.13.rest_3_), channel_id=1, source_target_pairs={{0,8},{1,9},{2,10},{3,11},{4,12},{5,13},{6,14},{7,15},{8,0},{9,1},... | collective-permute-start | bytes 3145736 | tf_op jit(solution)/shard_map/ppermute | solution.py:63
  168.3 28.3 %collective-permute-start.26 = (bf16[256,2048]{1,0:T(8,128)(2,1)}, bf16[256,2048]{1,0:T(8,128)(2,1)}, u32[]{:S(2)}, u32[]{:S(2)}) collective-permute-start(bf16[256,2048]{1,0:T(8,128)(2,1)} %fusion.5), channel_id=1, source_target_pairs={{0,16},{1,17},{2,18},{3,19},{4,20},{5,21},{6,22},{7,23},{8,12},{9,... | collective-permute-start | bytes 3145736 | tf_op jit(solution)/shard_map/ppermute | solution.py:93
  172.6 24.0 %collective-permute-start.25 = (bf16[256,2048]{1,0:T(8,128)(2,1)}, bf16[256,2048]{1,0:T(8,128)(2,1)}, u32[]{:S(2)}, u32[]{:S(2)}) collective-permute-start(bf16[256,2048]{1,0:T(8,128)(2,1)} %fusion.4), channel_id=1, source_target_pairs={{0,1},{1,16},{2,3},{3,18},{4,5},{5,20},{6,7},{7,22},{8,10},{9,11},... | collective-permute-start | bytes 3145736 | tf_op jit(solution)/shard_map/ppermute | solution.py:93
  177.0 19.6 %collective-permute-start.24 = (bf16[256,2048]{1,0:T(8,128)(2,1)}, bf16[256,2048]{1,0:T(8,128)(2,1)}, u32[]{:S(2)}, u32[]{:S(2)}) collective-permute-start(bf16[256,2048]{1,0:T(8,128)(2,1)} %fusion.3), channel_id=1, source_target_pairs={{0,17},{1,0},{2,19},{3,2},{4,21},{5,4},{6,23},{7,6},{8,14},{9,15},... | collective-permute-start | bytes 3145736 | tf_op jit(solution)/shard_map/ppermute | solution.py:93
  181.2 23.0 %collective-permute-start.17 = (bf16[256,1024]{1,0:T(8,128)(2,1)S(1)}, bf16[256,1024]{1,0:T(8,128)(2,1)S(1)}, u32[]{:S(2)}, u32[]{:S(2)}) collective-permute-start(bf16[256,1024]{1,0:T(8,128)(2,1)S(1)} %pad_maximum_fusion.3), channel_id=1, source_target_pairs={{0,8},{1,9},{2,10},{3,11},{4,12},{5,13},{6,14},{7,15},{8,0},{9,1},... | collective-permute-start | bytes 1572872 | tf_op jit(solution)/shard_map/ppermute | solution.py:63
  199.9 8.1 %collective-permute-start.29 = (bf16[256,512]{1,0:T(8,128)(2,1)S(1)}, bf16[256,512]{1,0:T(8,128)(2,1)S(1)}, u32[]{:S(2)}, u32[]{:S(2)}) collective-permute-start(bf16[256,512]{1,0:T(8,128)(2,1)S(1)} %get-tuple-element.60), channel_id=1, source_target_pairs={{0,64},{1,65},{2,66},{3,67},{4,68},{5,69},{6,70},{7,71},{8,24},{9,... | collective-permute-start | bytes 786440 | tf_op jit(solution)/shard_map/ppermute | solution.py:93
  201.0 9.7 %collective-permute-start.28 = (bf16[256,512]{1,0:T(8,128)(2,1)S(1)}, bf16[256,512]{1,0:T(8,128)(2,1)S(1)}, u32[]{:S(2)}, u32[]{:S(2)}) collective-permute-start(bf16[256,512]{1,0:T(8,128)(2,1)S(1)} %get-tuple-element.61), channel_id=1, source_target_pairs={{0,32},{1,33},{2,34},{3,35},{4,36},{5,37},{6,38},{7,39},{8,9},{9,2... | collective-permute-start | bytes 786440 | tf_op jit(solution)/shard_map/ppermute | solution.py:93
  202.0 8.7 %collective-permute-start.27 = (bf16[256,512]{1,0:T(8,128)(2,1)S(1)}, bf16[256,512]{1,0:T(8,128)(2,1)S(1)}, u32[]{:S(2)}, u32[]{:S(2)}) collective-permute-start(bf16[256,512]{1,0:T(8,128)(2,1)S(1)} %get-tuple-element.59), channel_id=1, source_target_pairs={{0,96},{1,97},{2,98},{3,99},{4,100},{5,101},{6,102},{7,103},{8,25}... | collective-permute-start | bytes 786440 | tf_op jit(solution)/shard_map/ppermute | solution.py:93
  210.9 11.1 %collective-permute-start.32 = (bf16[256,128]{1,0:T(8,128)(2,1)S(1)}, bf16[256,128]{1,0:T(8,128)(2,1)S(1)}, u32[]{:S(2)}, u32[]{:S(2)}) collective-permute-start(bf16[256,128]{1,0:T(8,128)(2,1)S(1)} %get-tuple-element.69), channel_id=1, source_target_pairs={{0,4},{1,5},{2,6},{3,7},{4,0},{5,1},{6,2},{7,3},{8,72},{9,73},{10,... | collective-permute-start | bytes 196616 | tf_op jit(solution)/shard_map/ppermute | solution.py:93
  217.9 5.5 %collective-permute-start.31 = (bf16[256,128]{1,0:T(8,128)(2,1)S(1)}, bf16[256,128]{1,0:T(8,128)(2,1)S(1)}, u32[]{:S(2)}, u32[]{:S(2)}) collective-permute-start(bf16[256,128]{1,0:T(8,128)(2,1)S(1)} %get-tuple-element.70), channel_id=1, source_target_pairs={{0,2},{1,3},{2,4},{3,5},{4,6},{5,7},{6,0},{7,1},{8,40},{9,41},{10,... | collective-permute-start | bytes 196616 | tf_op jit(solution)/shard_map/ppermute | solution.py:93
  (33 other events, 240.7 us)

commit v4 on v3

--- a/solution.py
+++ b/solution.py
@@ -127,12 +127,61 @@
             pl.BlockSpec((step_rows, features), lambda i: (i, 0)),
         ],
         out_specs=(half_spec, half_spec),
+        compiler_params=pltpu.CompilerParams(vmem_limit_bytes=16 << 20),
+        cost_estimate=pl.CostEstimate(
+            flops=0, bytes_accessed=4 * rows * features, transcendentals=0
+        ),
+        name="shuffle_tokens",
+    )(table, tokens)
+
+
+def weight_terms_kernel(grads, peer_grads, tokens, peer_tokens, *rest):
+    outs, turned = rest[:-1], rest[-1]
+    step = pl.program_id(0)
+
+    @pl.when(step == 0)
+    def _():
+        turned[0] = grads[...].T
+        turned[1] = peer_grads[...].T
+
+    term = jnp.dot(turned[0], tokens[...], preferred_element_type=jnp.float32) + jnp.dot(
+        turned[1], peer_tokens[...], preferred_element_type=jnp.float32
+    )
+    for n, out in enumerate(outs):
+
+        @pl.when(step // 2 == n)
+        def _(out=out):
+            out[...] = term.astype(out.dtype)
+
+
+def weight_terms(grads, peer_grads, tokens, peer_tokens):
+    rows, features = tokens.shape
+    both = grads.shape[1]
+    pieces = len(OFFSETS)
+    width = features // pieces // 2
+    whole = pl.BlockSpec((rows, both), lambda i: (0, 0))
+    cut = pl.BlockSpec((rows, width), lambda i: (0, i))
+    return pl.pallas_call(
+        weight_terms_kernel,
+        grid=(2 * pieces,),
+        out_shape=tuple(
+            jax.ShapeDtypeStruct((both, 2 * width), jnp.bfloat16 if n else jnp.float32)
+            for n in range(pieces)
+        ),
+        in_specs=[whole, whole, cut, cut],
+        out_specs=tuple(
+            pl.BlockSpec((both, width), lambda i, n=n: (0, jnp.clip(i - 2 * n, 0, 1)))
+            for n in range(pieces)
+        ),
+        scratch_shapes=[pltpu.VMEM((2, both, rows), jnp.bfloat16)],
         compiler_params=pltpu.CompilerParams(vmem_limit_bytes=56 << 20),
         cost_estimate=pl.CostEstimate(
-            flops=0, bytes_accessed=4 * rows * features, transcendentals=0
-        ),
-        name="shuffle_tokens",
-    )(table, tokens)
+            flops=4 * rows * both * features,
+            bytes_accessed=4 * rows * features + 3 * both * features,
+            transcendentals=0,
+        ),
+        name="weight_terms",
+    )(grads, peer_grads, tokens, peer_tokens)
 
 
 def token_grad_kernel(table, grads, *rest, count):
@@ -395,7 +444,7 @@
             pltpu.VMEM((query_blocks, columns, head_size), jnp.bfloat16),
             pltpu.SemaphoreType.DMA((5,)),
         ],
-        compiler_params=pltpu.CompilerParams(vmem_limit_bytes=40 << 20),
+        compiler_params=pltpu.CompilerParams(vmem_limit_bytes=26 << 20),
         cost_estimate=pl.CostEstimate(
             flops=28 * rows * heads * visible * head_size,
             bytes_accessed=8 * rows * width + 8 * length * head_size,
@@ -435,11 +484,7 @@
     latents = jnp.concatenate([latent_key, latent_value], axis=1)
     for phase in range(2):
         latents = jnp.concatenate(gather_ring(latents, phase), axis=0)
-    tokens_own, tokens_other = shuffle(table, token_rows)
-    latents, tokens_own, tokens_other, peer_both, meta = lax.optimization_barrier(
-        (latents, tokens_own, tokens_other, peer_both, meta)
-    )
-    tokens_peer = swap_cores(tokens_other)
+    latents, peer_both, meta = lax.optimization_barrier((latents, peer_both, meta))
     sums = jnp.broadcast_to(jnp.sum(jnp.abs(latents), axis=0, keepdims=True), (8, 2 * head_size))
     sums = sum(gather_ring(sums, 2))
     sums = sums + swap_cores(sums)
@@ -456,21 +501,19 @@
         ],
         axis=1,
     )
+    weights, shuffle_table = lax.optimization_barrier((weights, table))
     weight_parts = gather_ring(weights, 2)
+    tokens_own, tokens_other = shuffle(shuffle_table, token_rows)
+    other_parts = [swap_cores(part) for part in weight_parts]
     part_rows = weights.shape[0]
-
-    def project(rows):
-        total = 0.0
-        for i, part in enumerate(weight_parts):
-            total = total + jnp.dot(
-                rows[:, i * part_rows : (i + 1) * part_rows],
-                part,
-                preferred_element_type=jnp.float32,
+    projected = 0.0
+    for i, (own, other) in enumerate(zip(weight_parts, other_parts)):
+        cut = slice(i * part_rows, (i + 1) * part_rows)
+        for rows, part in ((tokens_own, own), (tokens_other, other)):
+            projected = projected + jnp.dot(
+                rows[:, cut], part, preferred_element_type=jnp.float32
             )
-        return total
-
-    peers_share = swap_cores(project(tokens_peer))
-    kv_here = (project(tokens_own) + peers_share).astype(jnp.bfloat16)
+    kv_here = projected.astype(jnp.bfloat16)
     groups = lax.axis_size(SAME_CORE_CTX)
     kv_same = lax.all_to_all(
         jnp.broadcast_to(kv_here[None], (groups,) + kv_here.shape).reshape(-1, 2 * head_size),
@@ -480,13 +523,13 @@
         tiled=True,
     )
     kv_other = swap_cores(kv_same)
-    other_parts = [swap_cores(part) for part in weight_parts]
+    tokens_peer = swap_cores(tokens_other)
 
     mixed, query_grad, same_terms, other_terms = attention(
         meta, queries[0], cotangent[0], peer_both, kv_same, kv_other, head_size, docs, blocks
     )
-    same_terms, other_terms, *other_parts = lax.optimization_barrier(
-        (same_terms, other_terms, *other_parts)
+    same_terms, other_terms, tokens_peer = lax.optimization_barrier(
+        (same_terms, other_terms, tokens_peer)
     )
     chip_terms = (same_terms + swap_cores(other_terms).astype(jnp.float32)).astype(jnp.bfloat16)
     terms = lax.all_to_all(chip_terms, SAME_CORE_CTX, split_axis=0, concat_axis=0, tiled=True)
@@ -495,16 +538,7 @@
     ).astype(jnp.bfloat16)
     peer_grads = swap_cores(grads)
 
-    def weight_term(i):
-        cut = slice(i * part_rows, (i + 1) * part_rows)
-        return sum(
-            lax.dot_general(
-                g, rows[:, cut], (((0,), (0,)), ((), ())), preferred_element_type=jnp.float32
-            )
-            for rows, g in ((tokens_own, grads), (tokens_peer, peer_grads))
-        )
-
-    summed = reduce_ring([weight_term(i) for i in range(4)], 2)
+    summed = reduce_ring(weight_terms(grads, peer_grads, tokens_own, tokens_peer), 2)
     token_grad = token_gradient(table, grads, weight_parts + other_parts)
     summed, token_grad = lax.optimization_barrier((summed, token_grad))
     from_peer = swap_cores(jnp.concatenate([mixed[rows_here:], query_grad[rows_here:]], axis=1))

time: 229 us -> 216 us (0.943); the launches traced: 225 us -> 216 us
  matrix products: 23.9 us -> 3.5 us
  starting transfers between devices: 41.9 us -> 34.2 us
  blocking collectives: 45.8 us -> 50.8 us
  waiting for transfers between devices: 52.6 us -> 56.7 us
  local copies, waits for them, and re-layouts: 14.8 us -> 18.8 us
  Pallas kernels: 36.9 us -> 40.8 us
  other arithmetic: 6.44 us -> 8.93 us
    dot_general x16 -> x8, matrix products: 23.9 us -> 3.5 us  [body(): jnp.dot(rows[:, cut], part, preferred_element_type=jnp.float32)]
    pallas_call x0 -> x1, Pallas kernels: none -> 10.1 us  [weight_terms(): pl.pallas_call(weight_terms_kernel, grid=(2 * pieces,), out_shape=tuple((...]
    ppermute x9, waiting for transfers between devices: 6.94 us -> 14.4 us  [reduce_ring(): lax.ppermute(piece.astype(jnp.bfloat16), AXES, along_ring(phase, offset))]
    ppermute x9, starting transfers between devices: 19 us -> 12.7 us  [reduce_ring(): lax.ppermute(piece.astype(jnp.bfloat16), AXES, along_ring(phase, offset))]
    pallas_call x1, Pallas kernels: 10.4 us -> 4.19 us  [shuffle(): pl.pallas_call(shuffle_kernel, grid=(rows // step_rows,), out_shape=(half...]
    all_to_all x1, blocking collectives: 24.9 us -> 30.3 us  [body(): lax.all_to_all(chip_terms, SAME_CORE_CTX, split_axis=0, concat_axis=0, ti...]
    unnamed x56 -> x64, local copies, waits for them, and re-layouts: 8.4 us -> 13 us
    ppermute x12, waiting for transfers between devices: 37.9 us -> 34 us  [gather_ring(): lax.ppermute(value, AXES, along_ring(phase, -offset))]
  transfers between devices with their start and end apart: 33 -> 32, of which waited for: 14 -> 20; matrix products, arithmetic and copies ran while one was open for 11% -> 6% of each run, Pallas kernels for 16% -> 14%
where the time goes in v4:
time: 216 us
  waiting for transfers between devices  56.7 us (26%)
  blocking collectives  50.8 us (24%)
  Pallas kernels  40.8 us (19%)
  starting transfers between devices  34.2 us (16%)
  local copies, waits for them, and re-layouts  18.8 us (9%)
  other arithmetic  8.93 us (4%)
  matrix products  3.5 us (2%)
  between operations  2.53 us (1%)
    ppermute x12, waiting for transfers between devices, gather_ring(): lax.ppermute(value, AXES, along_ring(phase, -offset))  34 us
    all_to_all x1, blocking collectives, body(): lax.all_to_all(chip_terms, SAME_CORE_CTX, split_axis=0, concat_axis=0, ti...  30.3 us
    all_to_all x1, blocking collectives, body(): lax.all_to_all(jnp.broadcast_to(kv_here[None], (groups,) + kv_here.shape)...  20.5 us
    ppermute x12, starting transfers between devices, gather_ring(): lax.ppermute(value, AXES, along_ring(phase, -offset))  19.8 us
    pallas_call x1, Pallas kernels, attention(): pl.pallas_call(functools.partial(attention_kernel, heads=heads, head_size...  16.8 us
    ppermute x9, waiting for transfers between devices, reduce_ring(): lax.ppermute(piece.astype(jnp.bfloat16), AXES, along_ring(phase, offset))  14.4 us
    unnamed x64, local copies, waits for them, and re-layouts  13 us
    ppermute x9, starting transfers between devices, reduce_ring(): lax.ppermute(piece.astype(jnp.bfloat16), AXES, along_ring(phase, offset))  12.7 us
  transfers between devices with their start and end apart: 32, of which 20 were waited for; matrix products, arithmetic and copies ran while one was open for 6% of the time, Pallas kernels for 14%

profile of v4, /device:TPU:0, one launch (start us, length us, event | category | flops | bytes accessed | tf_op | source)
XLA Modules:
  0.0 216.1 jit_solution(9557818219775176653)
XLA Ops:
  6.9 1.9 collective-permute-start.2
  10.4 3.2 %collective-permute-done.2 = f32[128,256]{1,0:T(8,128)S(1)} collective-permute-done((f32[128,256]{1,0:T(8,128)}, f32[128,256]{1,0:T(8,128)S(1)}, u32[]{:S(2)}, u32[]{:S(2)}) %collective-permute-start.2) | collective-permute-done | bytes 131104 | tf_op jit(solution)/shard_map/ppermute | solution.py:86
  18.0 2.1 collective-permute-start.5
  20.1 4.8 %collective-permute-done.3 = f32[512,256]{1,0:T(8,128)S(1)} collective-permute-done((f32[512,256]{1,0:T(8,128)S(1)}, f32[512,256]{1,0:T(8,128)S(1)}, u32[]{:S(2)}, u32[]{:S(2)}) %collective-permute-start.3) | collective-permute-done | bytes 524320 | tf_op jit(solution)/shard_map/ppermute | solution.py:86
  25.5 6.4 %collective-permute-done.5 = f32[512,256]{1,0:T(8,128)S(1)} collective-permute-done((f32[512,256]{1,0:T(8,128)S(1)}, f32[512,256]{1,0:T(8,128)S(1)}, u32[]{:S(2)}, u32[]{:S(2)}) %collective-permute-start.5) | collective-permute-done | bytes 524320 | tf_op jit(solution)/shard_map/ppermute | solution.py:86
  32.3 4.0 %collective-permute-start.9 = (f32[8,256]{1,0:T(8,128)S(1)}, f32[8,256]{1,0:T(8,128)S(1)}, u32[]{:S(2)}, u32[]{:S(2)}) collective-permute-start(f32[8,256]{1,0:T(8,128)S(1)} %broadcast_in_dim.53), channel_id=1, source_target_pairs={{0,16},{1,17},{2,18},{3,19},{4,20},{5,21},{6,22},{7,23},{8,12},{9,... | collective-permute-start | bytes 24584 | tf_op jit(solution)/shard_map/ppermute | solution.py:86
  39.9 1.9 collective-permute-done.7
  45.7 3.1 %collective-permute-start.14 = (bf16[2048,256]{1,0:T(8,128)(2,1)S(1)}, bf16[2048,256]{1,0:T(8,128)(2,1)S(1)}, u32[]{:S(2)}, u32[]{:S(2)}) collective-permute-start(bf16[2048,256]{1,0:T(8,128)(2,1)S(1)} %pad_maximum_fusion.rest_0_), channel_id=1, source_target_pairs={{0,17},{1,0},{2,19},{3,2},{4,21},{5,4},{6,23},{7,6},{8,14},{9,15},... | collective-permute-start | bytes 3145736 | tf_op jit(solution)/shard_map/ppermute | solution.py:86
  48.8 3.4 %copy-done = bf16[1,256,16384]{2,1,0:T(8,128)(2,1)S(1)} copy-done((bf16[1,256,16384]{2,1,0:T(8,128)(2,1)S(1)}, bf16[1,256,16384]{2,1,0:T(8,128)(2,1)}, u32[]{:S(2)}) %copy-start) | copy-done | bytes 8388632
  52.2 4.2 %shuffle_tokens.1 = (bf16[256,8192]{1,0:T(8,128)(2,1)S(1)}, bf16[256,8192]{1,0:T(8,128)(2,1)S(1)}) custom-call(s32[128]{0:T(128)S(1)} %fusion.17.table, bf16[256,16384]{1,0:T(8,128)(2,1)S(1)} %bitcast.30), custom_call_target="tpu_custom_call" | custom-call | bytes 16777216 | tf_op jit(solution)/shard_map/shuffle_tokens/pallas_call | solution.py:121
  57.4 15.4 %collective-permute-done.12.rest_1_ = bf16[2048,256]{1,0:T(8,128)(2,1)S(1)} collective-permute-done((bf16[2048,256]{1,0:T(8,128)(2,1)S(1)}, bf16[2048,256]{1,0:T(8,128)(2,1)S(1)}, u32[]{:S(2)}, u32[]{:S(2)}) %collective-permute-start.12) | collective-permute-done | bytes 1048608 | tf_op jit(solution)/shard_map/ppermute | solution.py:86
  79.1 20.5 %all_to_all.17 = bf16[8,256,256]{2,1,0:T(8,128)(2,1)S(1)} all-to-all(bf16[8,256,256]{2,1,0:T(8,128)(2,1)S(1)} %broadcast_in_dim.57), channel_id=1, replica_groups=mesh['y'=4,'zh'=2,'core'=2,'x'=4,'zl'=2] {'y','zh'}, dimensions={0} | all-to-all | bytes 2097152 | tf_op jit(solution)/shard_map/all_to_all | solution.py:518
  99.6 2.7 %collective-permute-done.18.kv_other = bf16[2048,256]{1,0:T(8,128)(2,1)S(1)} collective-permute-done((bf16[2048,256]{1,0:T(8,128)(2,1)S(1)}, bf16[2048,256]{1,0:T(8,128)(2,1)S(1)}, u32[]{:S(2)}, u32[]{:S(2)}) %collective-permute-start.18) | collective-permute-done | bytes 1048608 | tf_op jit(solution)/shard_map/ppermute | solution.py:63
  102.2 16.8 %masked_attention.1 = (bf16[512,512]{1,0:T(8,128)(2,1)S(1)}, bf16[512,512]{1,0:T(8,128)(2,1)S(1)}, f32[2048,256]{1,0:T(8,128)S(1)}, bf16[2048,256]{1,0:T(8,128)(2,1)S(1)}) custom-call(s32[42]{0:T(128)S(1)} %pad_add_fusion.meta, bf16[256,1024]{1,0:T(8,128)(2,1)S(1)} %bitcast.33, bf16[256,1024]{1,0:T(8,128)(2,1)S(1)} %bitcast.34, ...), custom_call_target="tpu_custom_call" | custom-call | flops 8455716864 | bytes 6291456 | tf_op jit(solution)/shard_map/masked_attention/pallas_call | solution.py:419
  119.3 2.5 %collective-permute-done.21 = bf16[2048,256]{1,0:T(8,128)(2,1)S(1)} collective-permute-done((bf16[2048,256]{1,0:T(8,128)(2,1)S(1)}, bf16[2048,256]{1,0:T(8,128)(2,1)S(1)}, u32[]{:S(2)}, u32[]{:S(2)}) %collective-permute-start.21) | collective-permute-done | bytes 1048608 | tf_op jit(solution)/shard_map/ppermute | solution.py:63
  122.1 30.3 %all_to_all.18 = bf16[8,256,256]{2,1,0:T(8,128)(2,1)} all-to-all(bf16[8,256,256]{2,1,0:T(8,128)(2,1)S(1)} %bitcast.36), channel_id=1, replica_groups=mesh['y'=4,'zh'=2,'core'=2,'x'=4,'zl'=2] {'y','zh'}, dimensions={0} | all-to-all | bytes 2097152 | tf_op jit(solution)/shard_map/all_to_all | solution.py:535
  155.8 10.1 %weight_terms.1 = (f32[256,2048]{1,0:T(8,128)}, bf16[256,2048]{1,0:T(8,128)(2,1)}, bf16[256,2048]{1,0:T(8,128)(2,1)}, bf16[256,2048]{1,0:T(8,128)(2,1)}) custom-call(bf16[256,256]{1,0:T(8,128)(2,1)} %copy-done.2, bf16[256,256]{1,0:T(8,128)(2,1)} %copy-done.24, bf16[256,8192]{1,0:T(8,128)(2,1)} %copy-done.1, bf16[256,8192]{1,0:T(8,128)(2,1)} %copy-done.22), custom_call_target="tpu_custom_call" | custom-call | flops 2147483648 | bytes 14680064 | tf_op jit(solution)/shard_map/weight_terms/pallas_call | solution.py:164
  177.5 9.7 %token_gradient.1 = bf16[256,16384]{1,0:T(8,128)(2,1)} custom-call(s32[128]{0:T(128)S(1)} %fusion.17.table, bf16[256,256]{1,0:T(8,128)(2,1)S(1)} %copy-done.3, bf16[2048,256]{1,0:T(8,128)(2,1)S(1)} %pad_maximum_fusion.rest_0_, bf16[2048,256]{1,0:T(8,128)(2,1)S(1)} %copy-done.5, bf16[2048,256]{1,0:T(8,128)(2,1)S(1)} %copy-done.7, ...), custom_call_target="tpu_custom_call" | custom-call | flops 2147483648 | bytes 16777216 | tf_op jit(solution)/shard_map/token_gradient/pallas_call | solution.py:220
  187.3 6.5 %collective-permute-done.24 = bf16[256,2048]{1,0:T(8,128)(2,1)} collective-permute-done((bf16[256,2048]{1,0:T(8,128)(2,1)}, bf16[256,2048]{1,0:T(8,128)(2,1)}, u32[]{:S(2)}, u32[]{:S(2)}) %collective-permute-start.24) | collective-permute-done | bytes 1048608 | tf_op jit(solution)/shard_map/ppermute | solution.py:93
  193.8 2.5 %convert_add_fusion = f32[256,2048]{1,0:T(8,128)S(1)} fusion(bf16[256,2048]{1,0:T(8,128)(2,1)} %collective-permute-done.25, bf16[256,2048]{1,0:T(8,128)(2,1)} %collective-permute-done.24, f32[256,2048]{1,0:T(8,128)S(1)} %copy-done.23, bf16[256,2048]{1,0:T(8,128)(2,1)} %collective-permute-done.23), kind=kLoop, calls=%fused_computation | loop fusion | flops 3145728 | bytes 7340032 | tf_op jit(solution)/shard_map/add | solution.py:94
  198.5 2.8 %collective-permute-start.26 = (bf16[256,512]{1,0:T(8,128)(2,1)S(1)}, bf16[256,512]{1,0:T(8,128)(2,1)S(1)}, u32[]{:S(2)}, u32[]{:S(2)}) collective-permute-start(bf16[256,512]{1,0:T(8,128)(2,1)S(1)} %get-tuple-element.61), channel_id=1, source_target_pairs={{0,96},{1,97},{2,98},{3,99},{4,100},{5,101},{6,102},{7,103},{8,25}... | collective-permute-start | bytes 786440 | tf_op jit(solution)/shard_map/ppermute | solution.py:93
  202.2 2.3 %collective-permute-done.28 = bf16[256,512]{1,0:T(8,128)(2,1)S(1)} collective-permute-done((bf16[256,512]{1,0:T(8,128)(2,1)S(1)}, bf16[256,512]{1,0:T(8,128)(2,1)S(1)}, u32[]{:S(2)}, u32[]{:S(2)}) %collective-permute-start.28) | collective-permute-done | bytes 262176 | tf_op jit(solution)/shard_map/ppermute | solution.py:93
  204.6 2.7 %collective-permute-done.27 = bf16[256,512]{1,0:T(8,128)(2,1)S(1)} collective-permute-done((bf16[256,512]{1,0:T(8,128)(2,1)S(1)}, bf16[256,512]{1,0:T(8,128)(2,1)S(1)}, u32[]{:S(2)}, u32[]{:S(2)}) %collective-permute-start.27) | collective-permute-done | bytes 262176 | tf_op jit(solution)/shard_map/ppermute | solution.py:93
  207.6 2.7 %collective-permute-start.30 = (bf16[256,128]{1,0:T(8,128)(2,1)S(1)}, bf16[256,128]{1,0:T(8,128)(2,1)S(1)}, u32[]{:S(2)}, u32[]{:S(2)}) collective-permute-start(bf16[256,128]{1,0:T(8,128)(2,1)S(1)} %get-tuple-element.72), channel_id=1, source_target_pairs={{0,2},{1,3},{2,4},{3,5},{4,6},{5,7},{6,0},{7,1},{8,40},{9,41},{10,... | collective-permute-start | bytes 196616 | tf_op jit(solution)/shard_map/ppermute | solution.py:93
  (149 shorter events, 51.1 us)
Async XLA Ops:
  3.6 6.6 %collective-permute-start = (f32[128,256]{1,0:T(8,128)}, f32[128,256]{1,0:T(8,128)S(1)}, u32[]{:S(2)}, u32[]{:S(2)}) collective-permute-start(f32[128,256]{1,0:T(8,128)} %get-tuple-element.75), channel_id=1, source_target_pairs={{0,2},{1,3},{2,4},{3,5},{4,6},{5,7},{6,0},{7,1},{8,40},{9,41},{10,... | collective-permute-start | bytes 393224 | tf_op jit(solution)/shard_map/ppermute | solution.py:86
  5.2 5.2 %collective-permute-start.1 = (f32[128,256]{1,0:T(8,128)}, f32[128,256]{1,0:T(8,128)S(1)}, u32[]{:S(2)}, u32[]{:S(2)}) collective-permute-start(f32[128,256]{1,0:T(8,128)} %get-tuple-element.75), channel_id=1, source_target_pairs={{0,6},{1,7},{2,0},{3,1},{4,2},{5,3},{6,4},{7,5},{8,104},{9,105},{1... | collective-permute-start | bytes 393224 | tf_op jit(solution)/shard_map/ppermute | solution.py:86
  6.9 6.7 %collective-permute-start.2 = (f32[128,256]{1,0:T(8,128)}, f32[128,256]{1,0:T(8,128)S(1)}, u32[]{:S(2)}, u32[]{:S(2)}) collective-permute-start(f32[128,256]{1,0:T(8,128)} %get-tuple-element.75), channel_id=1, source_target_pairs={{0,4},{1,5},{2,6},{3,7},{4,0},{5,1},{6,2},{7,3},{8,72},{9,73},{10,... | collective-permute-start | bytes 393224 | tf_op jit(solution)/shard_map/ppermute | solution.py:86
  10.1 21.8 %collective-permute-start.6 = (bf16[256,1024]{1,0:T(8,128)(2,1)S(1)}, bf16[256,1024]{1,0:T(8,128)(2,1)S(1)}, u32[]{:S(2)}, u32[]{:S(2)}) collective-permute-start(bf16[256,1024]{1,0:T(8,128)(2,1)S(1)} %pad_maximum_fusion.2), channel_id=1, source_target_pairs={{0,8},{1,9},{2,10},{3,11},{4,12},{5,13},{6,14},{7,15},{8,0},{9,1},... | collective-permute-start | bytes 1572872 | tf_op jit(solution)/shard_map/ppermute | solution.py:63
  14.5 10.5 %collective-permute-start.3 = (f32[512,256]{1,0:T(8,128)S(1)}, f32[512,256]{1,0:T(8,128)S(1)}, u32[]{:S(2)}, u32[]{:S(2)}) collective-permute-start(f32[512,256]{1,0:T(8,128)S(1)} %pad_maximum_fusion.1), channel_id=1, source_target_pairs={{0,32},{1,33},{2,34},{3,35},{4,36},{5,37},{6,38},{7,39},{8,9},{9,2... | collective-permute-start | bytes 1572872 | tf_op jit(solution)/shard_map/ppermute | solution.py:86
  16.3 9.2 %collective-permute-start.4 = (f32[512,256]{1,0:T(8,128)S(1)}, f32[512,256]{1,0:T(8,128)S(1)}, u32[]{:S(2)}, u32[]{:S(2)}) collective-permute-start(f32[512,256]{1,0:T(8,128)S(1)} %pad_maximum_fusion.1), channel_id=1, source_target_pairs={{0,96},{1,97},{2,98},{3,99},{4,100},{5,101},{6,102},{7,103},{8,25}... | collective-permute-start | bytes 1572872 | tf_op jit(solution)/shard_map/ppermute | solution.py:86
  18.0 13.9 %collective-permute-start.5 = (f32[512,256]{1,0:T(8,128)S(1)}, f32[512,256]{1,0:T(8,128)S(1)}, u32[]{:S(2)}, u32[]{:S(2)}) collective-permute-start(f32[512,256]{1,0:T(8,128)S(1)} %pad_maximum_fusion.1), channel_id=1, source_target_pairs={{0,64},{1,65},{2,66},{3,67},{4,68},{5,69},{6,70},{7,71},{8,24},{9,... | collective-permute-start | bytes 1572872 | tf_op jit(solution)/shard_map/ppermute | solution.py:86
  32.3 6.0 %collective-permute-start.9 = (f32[8,256]{1,0:T(8,128)S(1)}, f32[8,256]{1,0:T(8,128)S(1)}, u32[]{:S(2)}, u32[]{:S(2)}) collective-permute-start(f32[8,256]{1,0:T(8,128)S(1)} %broadcast_in_dim.53), channel_id=1, source_target_pairs={{0,16},{1,17},{2,18},{3,19},{4,20},{5,21},{6,22},{7,23},{8,12},{9,... | collective-permute-start | bytes 24584 | tf_op jit(solution)/shard_map/ppermute | solution.py:86
  36.9 4.9 %collective-permute-start.7 = (f32[8,256]{1,0:T(8,128)S(1)}, f32[8,256]{1,0:T(8,128)S(1)}, u32[]{:S(2)}, u32[]{:S(2)}) collective-permute-start(f32[8,256]{1,0:T(8,128)S(1)} %broadcast_in_dim.53), channel_id=1, source_target_pairs={{0,1},{1,16},{2,3},{3,18},{4,5},{5,20},{6,7},{7,22},{8,10},{9,11},... | collective-permute-start | bytes 24584 | tf_op jit(solution)/shard_map/ppermute | solution.py:86
  45.5 27.3 %collective-permute-start.12 = (bf16[2048,256]{1,0:T(8,128)(2,1)S(1)}, bf16[2048,256]{1,0:T(8,128)(2,1)S(1)}, u32[]{:S(2)}, u32[]{:S(2)}) collective-permute-start(bf16[2048,256]{1,0:T(8,128)(2,1)S(1)} %pad_maximum_fusion.rest_0_), channel_id=1, source_target_pairs={{0,1},{1,16},{2,3},{3,18},{4,5},{5,20},{6,7},{7,22},{8,10},{9,11},... | collective-permute-start | bytes 3145736 | tf_op jit(solution)/shard_map/ppermute | solution.py:86
  45.7 27.2 %collective-permute-start.14 = (bf16[2048,256]{1,0:T(8,128)(2,1)S(1)}, bf16[2048,256]{1,0:T(8,128)(2,1)S(1)}, u32[]{:S(2)}, u32[]{:S(2)}) collective-permute-start(bf16[2048,256]{1,0:T(8,128)(2,1)S(1)} %pad_maximum_fusion.rest_0_), channel_id=1, source_target_pairs={{0,17},{1,0},{2,19},{3,2},{4,21},{5,4},{6,23},{7,6},{8,14},{9,15},... | collective-permute-start | bytes 3145736 | tf_op jit(solution)/shard_map/ppermute | solution.py:86
  48.8 24.5 %collective-permute-start.16 = (bf16[2048,256]{1,0:T(8,128)(2,1)S(1)}, bf16[2048,256]{1,0:T(8,128)(2,1)S(1)}, u32[]{:S(2)}, u32[]{:S(2)}) collective-permute-start(bf16[2048,256]{1,0:T(8,128)(2,1)S(1)} %pad_maximum_fusion.rest_0_), channel_id=1, source_target_pairs={{0,16},{1,17},{2,18},{3,19},{4,20},{5,21},{6,22},{7,23},{8,12},{9,... | collective-permute-start | bytes 3145736 | tf_op jit(solution)/shard_map/ppermute | solution.py:86
  48.8 24.6 %collective-permute-start.11 = (bf16[2048,256]{1,0:T(8,128)(2,1)S(1)}, bf16[2048,256]{1,0:T(8,128)(2,1)S(1)}, u32[]{:S(2)}, u32[]{:S(2)}) collective-permute-start(bf16[2048,256]{1,0:T(8,128)(2,1)S(1)} %pad_maximum_fusion.rest_0_), channel_id=1, source_target_pairs={{0,8},{1,9},{2,10},{3,11},{4,12},{5,13},{6,14},{7,15},{8,0},{9,1},... | collective-permute-start | bytes 3145736 | tf_op jit(solution)/shard_map/ppermute | solution.py:63
  56.4 62.6 %collective-permute-start.20 = (bf16[256,8192]{1,0:T(8,128)(2,1)S(1)}, bf16[256,8192]{1,0:T(8,128)(2,1)S(1)}, u32[]{:S(2)}, u32[]{:S(2)}) collective-permute-start(bf16[256,8192]{1,0:T(8,128)(2,1)S(1)} %get-tuple-element.31), channel_id=1, source_target_pairs={{0,8},{1,9},{2,10},{3,11},{4,12},{5,13},{6,14},{7,15},{8,0},{9,1},... | collective-permute-start | bytes 12582920 | tf_op jit(solution)/shard_map/ppermute | solution.py:63
  73.4 5.1 %collective-permute-start.17 = (bf16[2048,256]{1,0:T(8,128)(2,1)S(1)}, bf16[2048,256]{1,0:T(8,128)(2,1)S(1)}, u32[]{:S(2)}, u32[]{:S(2)}) collective-permute-start(bf16[2048,256]{1,0:T(8,128)(2,1)S(1)} %collective-permute-done.16.rest_3_), channel_id=1, source_target_pairs={{0,8},{1,9},{2,10},{3,11},{4,12},{5,13},{6,14},{7,15},{8,0},{9,1},... | collective-permute-start | bytes 3145736 | tf_op jit(solution)/shard_map/ppermute | solution.py:63
  165.9 21.4 %collective-permute-start.25 = (bf16[256,2048]{1,0:T(8,128)(2,1)}, bf16[256,2048]{1,0:T(8,128)(2,1)}, u32[]{:S(2)}, u32[]{:S(2)}) collective-permute-start(bf16[256,2048]{1,0:T(8,128)(2,1)} %get-tuple-element.42), channel_id=1, source_target_pairs={{0,16},{1,17},{2,18},{3,19},{4,20},{5,21},{6,22},{7,23},{8,12},{9,... | collective-permute-start | bytes 3145736 | tf_op jit(solution)/shard_map/ppermute | solution.py:93
  167.2 26.6 %collective-permute-start.24 = (bf16[256,2048]{1,0:T(8,128)(2,1)}, bf16[256,2048]{1,0:T(8,128)(2,1)}, u32[]{:S(2)}, u32[]{:S(2)}) collective-permute-start(bf16[256,2048]{1,0:T(8,128)(2,1)} %get-tuple-element.41), channel_id=1, source_target_pairs={{0,1},{1,16},{2,3},{3,18},{4,5},{5,20},{6,7},{7,22},{8,10},{9,11},... | collective-permute-start | bytes 3145736 | tf_op jit(solution)/shard_map/ppermute | solution.py:93
  168.7 25.1 %collective-permute-start.23 = (bf16[256,2048]{1,0:T(8,128)(2,1)}, bf16[256,2048]{1,0:T(8,128)(2,1)}, u32[]{:S(2)}, u32[]{:S(2)}) collective-permute-start(bf16[256,2048]{1,0:T(8,128)(2,1)} %get-tuple-element.40), channel_id=1, source_target_pairs={{0,17},{1,0},{2,19},{3,2},{4,21},{5,4},{6,23},{7,6},{8,14},{9,15},... | collective-permute-start | bytes 3145736 | tf_op jit(solution)/shard_map/ppermute | solution.py:93
  172.5 28.8 %collective-permute-start.19 = (bf16[256,1024]{1,0:T(8,128)(2,1)S(1)}, bf16[256,1024]{1,0:T(8,128)(2,1)S(1)}, u32[]{:S(2)}, u32[]{:S(2)}) collective-permute-start(bf16[256,1024]{1,0:T(8,128)(2,1)S(1)} %pad_maximum_fusion.3), channel_id=1, source_target_pairs={{0,8},{1,9},{2,10},{3,11},{4,12},{5,13},{6,14},{7,15},{8,0},{9,1},... | collective-permute-start | bytes 1572872 | tf_op jit(solution)/shard_map/ppermute | solution.py:63
  196.5 8.1 %collective-permute-start.28 = (bf16[256,512]{1,0:T(8,128)(2,1)S(1)}, bf16[256,512]{1,0:T(8,128)(2,1)S(1)}, u32[]{:S(2)}, u32[]{:S(2)}) collective-permute-start(bf16[256,512]{1,0:T(8,128)(2,1)S(1)} %get-tuple-element.62), channel_id=1, source_target_pairs={{0,64},{1,65},{2,66},{3,67},{4,68},{5,69},{6,70},{7,71},{8,24},{9,... | collective-permute-start | bytes 786440 | tf_op jit(solution)/shard_map/ppermute | solution.py:93
  198.0 9.2 %collective-permute-start.27 = (bf16[256,512]{1,0:T(8,128)(2,1)S(1)}, bf16[256,512]{1,0:T(8,128)(2,1)S(1)}, u32[]{:S(2)}, u32[]{:S(2)}) collective-permute-start(bf16[256,512]{1,0:T(8,128)(2,1)S(1)} %get-tuple-element.63), channel_id=1, source_target_pairs={{0,32},{1,33},{2,34},{3,35},{4,36},{5,37},{6,38},{7,39},{8,9},{9,2... | collective-permute-start | bytes 786440 | tf_op jit(solution)/shard_map/ppermute | solution.py:93
  198.5 8.8 %collective-permute-start.26 = (bf16[256,512]{1,0:T(8,128)(2,1)S(1)}, bf16[256,512]{1,0:T(8,128)(2,1)S(1)}, u32[]{:S(2)}, u32[]{:S(2)}) collective-permute-start(bf16[256,512]{1,0:T(8,128)(2,1)S(1)} %get-tuple-element.61), channel_id=1, source_target_pairs={{0,96},{1,97},{2,98},{3,99},{4,100},{5,101},{6,102},{7,103},{8,25}... | collective-permute-start | bytes 786440 | tf_op jit(solution)/shard_map/ppermute | solution.py:93
  207.5 6.0 %collective-permute-start.31 = (bf16[256,128]{1,0:T(8,128)(2,1)S(1)}, bf16[256,128]{1,0:T(8,128)(2,1)S(1)}, u32[]{:S(2)}, u32[]{:S(2)}) collective-permute-start(bf16[256,128]{1,0:T(8,128)(2,1)S(1)} %get-tuple-element.71), channel_id=1, source_target_pairs={{0,4},{1,5},{2,6},{3,7},{4,0},{5,1},{6,2},{7,3},{8,72},{9,73},{10,... | collective-permute-start | bytes 196616 | tf_op jit(solution)/shard_map/ppermute | solution.py:93
  207.6 6.2 %collective-permute-start.30 = (bf16[256,128]{1,0:T(8,128)(2,1)S(1)}, bf16[256,128]{1,0:T(8,128)(2,1)S(1)}, u32[]{:S(2)}, u32[]{:S(2)}) collective-permute-start(bf16[256,128]{1,0:T(8,128)(2,1)S(1)} %get-tuple-element.72), channel_id=1, source_target_pairs={{0,2},{1,3},{2,4},{3,5},{4,6},{5,7},{6,0},{7,1},{8,40},{9,41},{10,... | collective-permute-start | bytes 196616 | tf_op jit(solution)/shard_map/ppermute | solution.py:93
  (36 other events, 258.7 us)
